TPU v7x, 256 devices: a whole 4x4x8 slice. The times are simulated.
256 devices in a mesh: snap: 16 (over z, x_hi), mesh: 16 (over x_lo, y, core).
Axes of the slice: x: 4 (x_hi: 2, x_lo: 2; x = x_hi * 2 + x_lo), y: 4, z: 8, core: 2. Of those that a mesh axis runs over, the one named last changes fastest.
Arguments:
- snapshots: float32 [49152, 2048], P('mesh', 'snap'), may hold values from -6 to 6
- region_ids: int32 [96, 512], P('mesh'), may hold values from 0 to 7
- conductivity: float32 [8], replicated, may hold values from 0.2 to 5
Outputs:
- gram: float32 [2048, 2048], P('snap', 'mesh')
All inputs are finite; a program needn't handle non-finite values.
Results may differ from a plain program's by a relative error of at most 0.0003.
Values sent between devices are 32-bit elements; how exact they have to be, the bound alone decides.
A program may use at most 128 MiB of HBM per device.

v0:
```python
import math

import jax
import jax.numpy as jnp
from jax import lax
from jax.sharding import PartitionSpec as P


def passed_along(value, axis, steps):
    count = lax.axis_size(axis)
    first, last = (max(0, -steps), min(count, count - steps))
    return lax.ppermute(value, axis, [(source, source + steps) for source in range(first, last)])


def weights_of(region_ids, conductivity):
    table = jnp.arange(conductivity.shape[0], dtype=jnp.int32)
    picked = jnp.where(
        region_ids[:, :, None] == table[None, None, :],
        conductivity[None, None, :],
        jnp.zeros((), conductivity.dtype),
    )
    return jnp.sum(picked, axis=-1) / 36.0


def element_terms(field, below, weight):
    lower = jnp.concatenate([field, below[None]], 0)
    padded = jnp.pad(lower, ((0, 0), (0, 1), (0, 0)))
    corner_a = padded[:-1, :-1]
    corner_b = padded[:-1, 1:]
    corner_e = padded[1:, :-1]
    corner_d = padded[1:, 1:]
    scaled = weight[:, :, None]
    to_a = scaled * (4.0 * corner_a + 2.0 * corner_b + 2.0 * corner_e + corner_d)
    to_b = scaled * (2.0 * corner_a + 4.0 * corner_b + corner_e + 2.0 * corner_d)
    to_e = scaled * (2.0 * corner_a + corner_b + 4.0 * corner_e + 2.0 * corner_d)
    to_d = scaled * (corner_a + 2.0 * corner_b + 2.0 * corner_e + 4.0 * corner_d)
    total = jnp.pad(to_a, ((0, 1), (0, 1), (0, 0))) + jnp.pad(to_b, ((0, 1), (1, 0), (0, 0)))
    total = (
        total + jnp.pad(to_e, ((1, 0), (0, 1), (0, 0))) + jnp.pad(to_d, ((1, 0), (1, 0), (0, 0)))
    )
    return total


def contract(left, right):
    return lax.dot_general(
        left,
        right,
        (((0,), (0,)), ((), ())),
        precision=lax.Precision.HIGHEST,
        preferred_element_type=jnp.float32,
    )


def local(snapshots, region_ids, conductivity):
    strip, width = region_ids.shape
    node_rows, group_cols = snapshots.shape
    field = snapshots.reshape(strip, width, group_cols)
    weight = weights_of(region_ids, conductivity)
    below = passed_along(field[0], "mesh", -1)
    total = element_terms(field, below, weight)
    carried = passed_along(total[strip, :width], "mesh", 1)
    inner = total[:strip, :width]
    panel = jnp.concatenate([inner[:1] + carried[None], inner[1:]], 0).reshape(
        node_rows, group_cols
    )
    partial_value = contract(snapshots, lax.all_gather(panel, "snap", axis=1, tiled=True))
    summed = lax.psum_scatter(partial_value, "mesh", scatter_dimension=1, tiled=True)
    total_nodes = node_rows * lax.axis_size("mesh")
    return summed / math.sqrt(total_nodes)


def solution(mesh):
    return jax.shard_map(
        local,
        mesh=mesh,
        in_specs=(P("mesh", "snap"), P("mesh", None), P()),
        out_specs=P("snap", "mesh"),
        check_vma=False,
    )
```

profile of v0, /device:TPU:31, one launch (start us, length us, event | category | flops | bytes accessed | tf_op | source)
XLA Modules:
  0.0 474.3 jit_solution(9330290577570268332)
XLA Ops:
  6.5 0.0 all-gather.2.cloned.1.call-start
  6.5 1.0 slice.28
  7.5 2.6 collective-permute-start
  10.1 0.8 select_reduce_fusion
  11.0 0.3 collective-permute-done
  11.2 0.0 copy-start
  11.2 1.6 pad_maximum_fusion
  12.9 0.2 copy-done
  13.1 0.6 add_multiply_fusion.3
  13.8 1.3 add_multiply_fusion.2
  15.1 1.3 collective-permute-start.1
  16.4 0.3 pad_add_fusion
  16.7 4.2 collective-permute-done.1
  20.9 0.1 add_add_fusion
  21.0 1.3 pad_maximum_fusion.1
  22.3 0.0 all-gather.2.cloned.1.call-update
  22.3 0.0 reduce-scatter.2.cloned.1.call-start
  22.4 338.4 %all-gather.2.cloned.1.call-done = f32[3072,2048]{1,0:T(8,128)} async-done(((f32[3072,128]{1,0:T(8,128)}), f32[3072,2048]{1,0:T(8,128)}) %all-gather.2.cloned.1.call-update) | async-done | bytes 25165840 | tf_op jit(solution)/shard_map/all_gather | solution.py:66
  360.8 43.1 %convolution_bitcast_fusion = f32[128,2048]{0,1:T(8,128)} fusion(f32[3072,2048]{1,0:T(8,128)} %all-gather.2.cloned.1.call-done, f32[3072,128]{1,0:T(8,128)S(1)} %copy-done), kind=kOutput, calls=%fused_computation.2 | convolution fusion | flops 9663676416 | bytes 27787264 | tf_op jit(solution)/shard_map/dot_general | solution.py:45
  403.9 0.0 reduce-scatter.2.cloned.1.call-update
  403.9 62.0 %reduce-scatter.2.cloned.1.call-done = f32[128,128]{0,1:T(8,128)} async-done(((f32[128,2048]{0,1:T(8,128)}), f32[128,128]{0,1:T(8,128)}) %reduce-scatter.2.cloned.1.call-update) | async-done | bytes 65552 | tf_op jit(solution)/shard_map/reduce_scatter | solution.py:67
  465.9 0.8 broadcast_multiply_fusion
  466.8 0.7 copy.5
  (2 shorter events, 0.0 us)
Async XLA Ops:
  6.5 354.2 %all-gather.2.cloned.1.call-start = ((), (), s32[]{:S(2)}) async-start(), calls=%async_computation.1 | async-start | bytes 26738688 | tf_op jit(solution)/shard_map/all_gather | solution.py:66
  7.5 3.7 collective-permute-start
  11.2 1.9 copy-start
  15.1 5.8 %collective-permute-start.1 = (f32[512,128]{1,0:T(8,128)S(1)}, f32[512,128]{1,0:T(8,128)S(1)}, u32[]{:S(2)}, u32[]{:S(2)}) collective-permute-start(f32[512,128]{1,0:T(8,128)S(1)} %add_bitcast_fusion), channel_id=1, source_target_pairs={{0,1},{1,2},{2,3},{3,4},{4,5},{5,6},{6,7},{7,8},{8,9},{9,10},{10,1... | collective-permute-start | bytes 786440 | tf_op jit(solution)/shard_map/ppermute | solution.py:12
  22.3 443.6 %reduce-scatter.2.cloned.1.call-start = ((), (), s32[]{:S(2)}) async-start(), calls=%async_computation.2 | async-start | bytes 1114112 | tf_op jit(solution)/shard_map/reduce_scatter | solution.py:67
Sparse Core Ops, SparseCore 0:
  22.4 338.2 all-gather.1
  404.0 61.8 reduce-scatter.1
where the time goes:
time: 477 us; the launch traced here: 474 us
  waiting for transfers between devices  405 us (85%)
  matrix products  43.1 us (9%)
  between operations  13.5 us (3%)
  other arithmetic  6.95 us (1%)
    all_gather x1, waiting for transfers between devices, local(): lax.all_gather(panel, 'snap', axis=1, tiled=True)  338 us
    reduce_scatter x1, waiting for transfers between devices, local(): lax.psum_scatter(partial_value, 'mesh', scatter_dimension=1, tiled=True)  62 us
    dot_general x1, matrix products, contract(): lax.dot_general(left, right, (((0,), (0,)), ((), ())), precision=lax.Prec...  43.1 us
  transfers between devices with their start and end apart: 4, of which 4 were waited for; matrix products, arithmetic and copies ran while one was open for 0% of the time, Pallas kernels for 0%

commit v1 on v0

--- a/solution.py
+++ b/solution.py
@@ -3,6 +3,7 @@
 import jax
 import jax.numpy as jnp
 from jax import lax
+from jax.sharding import Mesh
 from jax.sharding import PartitionSpec as P
 
 
@@ -54,6 +55,8 @@
 def local(snapshots, region_ids, conductivity):
     strip, width = region_ids.shape
     node_rows, group_cols = snapshots.shape
+    side = lax.axis_size("c")
+    tiles = lax.axis_size("mesh")
     field = snapshots.reshape(strip, width, group_cols)
     weight = weights_of(region_ids, conductivity)
     below = passed_along(field[0], "mesh", -1)
@@ -63,17 +66,35 @@
     panel = jnp.concatenate([inner[:1] + carried[None], inner[1:]], 0).reshape(
         node_rows, group_cols
     )
-    partial_value = contract(snapshots, lax.all_gather(panel, "snap", axis=1, tiled=True))
-    summed = lax.psum_scatter(partial_value, "mesh", scatter_dimension=1, tiled=True)
-    total_nodes = node_rows * lax.axis_size("mesh")
-    return summed / math.sqrt(total_nodes)
+    rows = lax.all_gather(snapshots, "c", axis=1, tiled=True)
+    cols = lax.all_gather(panel, "r", axis=1, tiled=True)
+    partial_value = contract(rows, cols)
+    pieces = (
+        partial_value.reshape(side, group_cols, side, group_cols)
+        .transpose(0, 2, 1, 3)
+        .reshape(side * side, group_cols, group_cols)
+    )
+    summed = lax.psum_scatter(pieces, "mesh", scatter_dimension=0, tiled=True)[0]
+    perm = []
+    for c in range(side):
+        for t in range(tiles):
+            dest_c, dest_t = t // side, c + side * (t % side)
+            perm.append((c * tiles + t, dest_c * tiles + dest_t))
+    placed = lax.ppermute(summed, ("c", "mesh"), perm)
+    total_nodes = node_rows * tiles
+    return placed / math.sqrt(total_nodes)
 
 
 def solution(mesh):
+    snap = mesh.shape["snap"]
+    side = math.isqrt(snap)
+    grid = Mesh(
+        mesh.devices.reshape(snap // side, side, mesh.shape["mesh"]), ("r", "c", "mesh")
+    )
     return jax.shard_map(
         local,
-        mesh=mesh,
-        in_specs=(P("mesh", "snap"), P("mesh", None), P()),
-        out_specs=P("snap", "mesh"),
+        mesh=grid,
+        in_specs=(P("mesh", ("r", "c")), P("mesh", None), P()),
+        out_specs=P(("r", "c"), "mesh"),
         check_vma=False,
     )

time: 477 us -> 354 us (0.74)
  waiting for transfers between devices: 405 us -> 309 us
  matrix products: 43.1 us -> 12.7 us
    all_gather x1 -> x2, waiting for transfers between devices: 338 us -> 238 us  [the longest x1 130 us: local(): cols = lax.all_gather(panel, 'r', axis=1, tiled=True)]
    dot_general x1, matrix products: 43.1 us -> 12.7 us  [contract(): lax.dot_general(left, right, (((0,), (0,)), ((), ())), precision=lax.Prec...]
  transfers between devices with their start and end apart: 4 -> 6, of which waited for: 4 -> 6; matrix products, arithmetic and copies ran while one was open for 0% -> 1% of each run, Pallas kernels for 0% -> 0%
where the time goes in v1:
time: 354 us; the launch traced here: 347 us
  waiting for transfers between devices  309 us (87%)
  between operations  13.2 us (4%)
  matrix products  12.7 us (4%)
  starting transfers between devices  5.88 us (2%)
  other arithmetic  4.42 us (1%)
    all_gather x1, waiting for transfers between devices, local(): cols = lax.all_gather(panel, 'r', axis=1, tiled=True)  130 us
    all_gather x1, waiting for transfers between devices, local(): rows = lax.all_gather(snapshots, 'c', axis=1, tiled=True)  108 us
    reduce_scatter x1, waiting for transfers between devices, local(): lax.psum_scatter(pieces, 'mesh', scatter_dimension=0, tiled=True)[0]  60.4 us
    dot_general x1, matrix products, contract(): lax.dot_general(left, right, (((0,), (0,)), ((), ())), precision=lax.Prec...  12.7 us
  transfers between devices with their start and end apart: 6, of which 6 were waited for; matrix products, arithmetic and copies ran while one was open for 1% of the time, Pallas kernels for 0%

profile of v1, /device:TPU:31, one launch (start us, length us, event | category | flops | bytes accessed | tf_op | source)
XLA Modules:
  0.0 347.2 jit_solution(13176668899420471793)
XLA Ops:
  6.5 0.0 copy-start
  6.5 0.0 copy-start.1
  6.5 0.0 copy-start.2
  6.5 0.0 all-gather.5.cloned.1.call-start
  6.5 0.7 all-gather.5.cloned.1.call-update
  7.3 0.0 all-gather.3.cloned.1.call-start
  7.3 0.6 copy-done
  8.0 2.6 collective-permute-start
  10.6 0.0 copy-done.1
  10.6 0.0 copy-done.2
  10.6 0.1 select_reduce_fusion
  10.7 1.0 collective-permute-done
  11.7 0.1 pad_maximum_fusion
  11.8 0.7 add_multiply_fusion.3
  12.5 1.3 add_multiply_fusion.2
  13.8 1.3 collective-permute-start.1
  15.1 0.3 pad_add_fusion
  15.4 4.2 %collective-permute-done.1 = f32[512,128]{1,0:T(8,128)S(1)} collective-permute-done((f32[512,128]{1,0:T(8,128)S(1)}, f32[512,128]{1,0:T(8,128)S(1)}, u32[]{:S(2)}, u32[]{:S(2)}) %collective-permute-start.1) | collective-permute-done | bytes 262176 | tf_op jit(solution)/shard_map/ppermute | solution.py:13
  19.6 0.1 add_add_fusion
  19.7 1.3 pad_maximum_fusion.1
  20.9 0.0 all-gather.3.cloned.1.call-update
  21.0 0.0 reduce-scatter.2.cloned.1.call-start
  21.0 108.2 %all-gather.5.cloned.1.call-done = f32[3072,512]{1,0:T(8,128)} async-done(((f32[3072,128]{1,0:T(8,128)}), f32[3072,512]{1,0:T(8,128)}) %all-gather.5.cloned.1.call-update) | async-done | bytes 6291472 | tf_op jit(solution)/shard_map/all_gather | solution.py:69
  129.2 129.5 %all-gather.3.cloned.1.call-done = f32[3072,512]{1,0:T(8,128)} async-done(((f32[3072,128]{1,0:T(8,128)}), f32[3072,512]{1,0:T(8,128)}) %all-gather.3.cloned.1.call-update) | async-done | bytes 6291472 | tf_op jit(solution)/shard_map/all_gather | solution.py:70
  258.8 12.7 %convolution_bitcast_fusion = f32[512,512]{0,1:T(8,128)S(1)} fusion(f32[3072,512]{1,0:T(8,128)} %all-gather.3.cloned.1.call-done, f32[3072,512]{1,0:T(8,128)} %all-gather.5.cloned.1.call-done), kind=kOutput, calls=%fused_computation.11 | convolution fusion | flops 9663676416 | bytes 13631488 | tf_op jit(solution)/shard_map/dot_general | solution.py:46
  271.5 0.4 reshape.21
  271.9 1.3 copy.5
  273.2 0.0 reduce-scatter.2.cloned.1.call-update
  273.2 60.4 %reduce-scatter.2.cloned.1.call-done = f32[1,128,128]{2,1,0:T(8,128)} async-done(((f32[16,128,128]{2,1,0:T(8,128)}), f32[1,128,128]{2,1,0:T(8,128)}) %reduce-scatter.2.cloned.1.call-update) | async-done | bytes 65552 | tf_op jit(solution)/shard_map/reduce_scatter | solution.py:77
  333.7 1.9 collective-permute-start.2
  335.6 4.5 %collective-permute-done.2 = f32[128,128]{1,0:T(8,128)S(1)} collective-permute-done((f32[128,128]{1,0:T(8,128)}, f32[128,128]{1,0:T(8,128)S(1)}, u32[]{:S(2)}, u32[]{:S(2)}) %collective-permute-start.2) | collective-permute-done | bytes 65568 | tf_op jit(solution)/shard_map/ppermute | solution.py:83
  340.1 0.6 broadcast_multiply_fusion
  (3 shorter events, 0.1 us)
Async XLA Ops:
  6.5 1.4 copy-start
  6.5 4.0 %copy-start.1 = (s32[6,512]{1,0:T(8,128)S(1)}, s32[6,512]{1,0:T(8,128)}, u32[]{:S(2)}) copy-start(s32[6,512]{1,0:T(8,128)} %param.4) | copy-start | bytes 36868
  6.5 4.0 %copy-start.2 = (f32[8]{0:T(128)S(1)}, f32[8]{0:T(128)}, u32[]{:S(2)}) copy-start(f32[8]{0:T(128)} %param.5) | copy-start | bytes 100
  6.5 122.7 %all-gather.5.cloned.1.call-start = ((), (), s32[]{:S(2)}) async-start(), calls=%async_computation.2 | async-start | bytes 7864320 | tf_op jit(solution)/shard_map/all_gather | solution.py:69
  7.3 251.5 %all-gather.3.cloned.1.call-start = ((), (), s32[]{:S(2)}) async-start(), calls=%async_computation.1 | async-start | bytes 7864320 | tf_op jit(solution)/shard_map/all_gather | solution.py:70
  8.0 3.7 %collective-permute-start = (f32[512,128]{1,0:T(8,128)S(1)}, f32[512,128]{1,0:T(8,128)S(1)}, u32[]{:S(2)}, u32[]{:S(2)}) collective-permute-start(f32[512,128]{1,0:T(8,128)S(1)} %slice.28), channel_id=1, source_target_pairs={{1,0},{2,1},{3,2},{4,3},{5,4},{6,5},{7,6},{8,7},{9,8},{10,9},{11,1... | collective-permute-start | bytes 786440 | tf_op jit(solution)/shard_map/ppermute | solution.py:13
  13.8 5.8 %collective-permute-start.1 = (f32[512,128]{1,0:T(8,128)S(1)}, f32[512,128]{1,0:T(8,128)S(1)}, u32[]{:S(2)}, u32[]{:S(2)}) collective-permute-start(f32[512,128]{1,0:T(8,128)S(1)} %add_bitcast_fusion), channel_id=1, source_target_pairs={{0,1},{1,2},{2,3},{3,4},{4,5},{5,6},{6,7},{7,8},{8,9},{9,10},{10,1... | collective-permute-start | bytes 786440 | tf_op jit(solution)/shard_map/ppermute | solution.py:13
  21.0 312.7 %reduce-scatter.2.cloned.1.call-start = ((), (), s32[]{:S(2)}) async-start(), calls=%async_computation.3 | async-start | bytes 1114112 | tf_op jit(solution)/shard_map/reduce_scatter | solution.py:77
  333.7 6.4 %collective-permute-start.2 = (f32[128,128]{1,0:T(8,128)}, f32[128,128]{1,0:T(8,128)S(1)}, u32[]{:S(2)}, u32[]{:S(2)}) collective-permute-start(f32[128,128]{1,0:T(8,128)} %bitcast.24), channel_id=1, source_target_pairs={{0,0},{1,4},{2,8},{3,12},{4,16},{5,20},{6,24},{7,28},{8,32},{9,36}... | collective-permute-start | bytes 196616 | tf_op jit(solution)/shard_map/ppermute | solution.py:83
Sparse Core Ops, SparseCore 0:
  9.2 120.0 all-gather.4
  131.0 127.6 all-gather.2
  273.4 60.2 reduce-scatter.1

commit v2 on v1

--- a/solution.py
+++ b/solution.py
@@ -52,6 +52,25 @@
     )
 
 
+def ring_gather(block, axis):
+    count = lax.axis_size(axis)
+    held = [block]
+    for shift in range(1, count):
+        held.append(lax.ppermute(block, axis, [(i, (i + shift) % count) for i in range(count)]))
+    return jnp.concatenate(held, 1)
+
+
+def direct_reduce_scatter(piece_of, axis):
+    count = lax.axis_size(axis)
+    me = lax.axis_index(axis)
+    total = piece_of(me)
+    for shift in range(1, count):
+        total = total + lax.ppermute(
+            piece_of((me + shift) % count), axis, [(i, (i + shift) % count) for i in range(count)]
+        )
+    return total
+
+
 def local(snapshots, region_ids, conductivity):
     strip, width = region_ids.shape
     node_rows, group_cols = snapshots.shape
@@ -66,15 +85,19 @@
     panel = jnp.concatenate([inner[:1] + carried[None], inner[1:]], 0).reshape(
         node_rows, group_cols
     )
-    rows = lax.all_gather(snapshots, "c", axis=1, tiled=True)
-    cols = lax.all_gather(panel, "r", axis=1, tiled=True)
+    rows = ring_gather(snapshots, "c")
+    cols = ring_gather(panel, "r")
     partial_value = contract(rows, cols)
-    pieces = (
-        partial_value.reshape(side, group_cols, side, group_cols)
-        .transpose(0, 2, 1, 3)
-        .reshape(side * side, group_cols, group_cols)
-    )
-    summed = lax.psum_scatter(pieces, "mesh", scatter_dimension=0, tiled=True)[0]
+    me_r, me_c = lax.axis_index("r"), lax.axis_index("c")
+
+    def piece_of(t):
+        row_block = (me_c - t // side) % side
+        col_block = (me_r - t % side) % side
+        return lax.dynamic_slice(
+            partial_value, (row_block * group_cols, col_block * group_cols), (group_cols, group_cols)
+        )
+
+    summed = direct_reduce_scatter(piece_of, "mesh")
     perm = []
     for c in range(side):
         for t in range(tiles):

time: 354 us -> 321 us (0.907)
  the two profiles are of different devices: /device:TPU:31 before, /device:TPU:89 now
where the time goes in v2:
time: 321 us
  waiting for transfers between devices  259 us (81%)
  starting transfers between devices  40.2 us (13%)
  matrix products  13.8 us (4%)
  other arithmetic  6.41 us (2%)
    ppermute x6, waiting for transfers between devices, ring_gather(): lax.ppermute(block, axis, [(i, (i + shift) % count) for i in range(count)])  198 us
    ppermute x2, waiting for transfers between devices, passed_along(): lax.ppermute(value, axis, [(source, source + steps) for source in range(f...  51 us
    ppermute x15, starting transfers between devices, direct_reduce_scatter(): lax.ppermute(piece_of((me + shift) % count), axis, [(i, (i + shift) % cou...  21.5 us
    dot_general x1, matrix products, contract(): lax.dot_general(left, right, (((0,), (0,)), ((), ())), precision=lax.Prec...  13.8 us
    ppermute x6, starting transfers between devices, ring_gather(): lax.ppermute(block, axis, [(i, (i + shift) % count) for i in range(count)])  12 us
    ppermute x1, waiting for transfers between devices, local(): placed = lax.ppermute(summed, ('c', 'mesh'), perm)  7.59 us
  transfers between devices with their start and end apart: 24, of which 10 were waited for; matrix products, arithmetic and copies ran while one was open for 2% of the time, Pallas kernels for 0%

profile of v2, /device:TPU:89, one launch (start us, length us, event | category | flops | bytes accessed | tf_op | source)
XLA Modules:
  0.0 321.0 jit_solution(958097119918676453)
XLA Ops:
  0.0 2.7 collective-permute-start
  2.7 1.0 slice.28
  3.7 2.9 collective-permute-start.3
  6.6 0.8 select_reduce_fusion
  7.5 49.8 %collective-permute-done.3 = f32[512,128]{1,0:T(8,128)S(1)} collective-permute-done((f32[512,128]{1,0:T(8,128)S(1)}, f32[512,128]{1,0:T(8,128)S(1)}, u32[]{:S(2)}, u32[]{:S(2)}) %collective-permute-start.3) | collective-permute-done | bytes 262176 | tf_op jit(solution)/shard_map/ppermute | solution.py:13
  57.2 1.6 pad_maximum_fusion
  59.1 0.6 add_multiply_fusion.3
  59.8 1.3 add_multiply_fusion.2
  61.1 1.9 collective-permute-start.4
  63.0 1.7 collective-permute-start.1
  65.0 1.3 collective-permute-done.4
  66.5 4.3 %collective-permute-start.5 = (f32[3072,128]{1,0:T(8,128)S(1)}, f32[3072,128]{1,0:T(8,128)}, u32[]{:S(2)}, u32[]{:S(2)}) collective-permute-start(f32[3072,128]{1,0:T(8,128)S(1)} %bitcast.10), channel_id=1, source_target_pairs={{0,64},{64,128},{128,192},{192,0},{1,65},{65,129},{129,193},{193,1... | collective-permute-start | bytes 4718600 | tf_op jit(solution)/shard_map/ppermute | solution.py:59
  70.7 1.0 collective-permute-start.6
  71.8 2.3 collective-permute-start.7
  74.0 58.7 %collective-permute-done.1 = f32[3072,128]{1,0:T(8,128)} collective-permute-done((f32[3072,128]{1,0:T(8,128)S(1)}, f32[3072,128]{1,0:T(8,128)}, u32[]{:S(2)}, u32[]{:S(2)}) %collective-permute-start.1) | collective-permute-done | bytes 1572896 | tf_op jit(solution)/shard_map/ppermute | solution.py:59
  132.7 32.7 %collective-permute-done.2 = f32[3072,128]{1,0:T(8,128)} collective-permute-done((f32[3072,128]{1,0:T(8,128)S(1)}, f32[3072,128]{1,0:T(8,128)}, u32[]{:S(2)}, u32[]{:S(2)}) %collective-permute-start.2) | collective-permute-done | bytes 1572896 | tf_op jit(solution)/shard_map/ppermute | solution.py:59
  165.4 34.1 %collective-permute-done.5 = f32[3072,128]{1,0:T(8,128)} collective-permute-done((f32[3072,128]{1,0:T(8,128)S(1)}, f32[3072,128]{1,0:T(8,128)}, u32[]{:S(2)}, u32[]{:S(2)}) %collective-permute-start.5) | collective-permute-done | bytes 1572896 | tf_op jit(solution)/shard_map/ppermute | solution.py:59
  199.5 72.1 %collective-permute-done.6 = f32[3072,128]{1,0:T(8,128)} collective-permute-done((f32[3072,128]{1,0:T(8,128)S(1)}, f32[3072,128]{1,0:T(8,128)}, u32[]{:S(2)}, u32[]{:S(2)}) %collective-permute-start.6) | collective-permute-done | bytes 1572896 | tf_op jit(solution)/shard_map/ppermute | solution.py:59
  271.6 13.8 %fusion = f32[512,512]{1,0:T(8,128)S(1)} fusion(f32[3072,128]{1,0:T(8,128)} %collective-permute-done.2, f32[3072,128]{1,0:T(8,128)} %collective-permute-done.1, f32[3072,128]{1,0:T(8,128)} %collective-permute-done, f32[3072,128]{1,0:T(8,128)S(1)} %copy-done, f32[3072,128]{1,0:T(8,128)} %collective-permute-done.7, f32[3072,128]{1,0:T(8,128)} %collective-permute-done.6, ...), kind=kOutput, calls=%fused_computation | convolution fusion | flops 9673113600 | bytes 13631488 | tf_op jit(solution)/shard_map/dot_general | solution.py:46
  286.0 5.0 %collective-permute-start.13 = (f32[128,128]{1,0:T(8,128)S(1)}, f32[128,128]{1,0:T(8,128)S(1)}, u32[]{:S(2)}, u32[]{:S(2)}) collective-permute-start(f32[128,128]{1,0:T(8,128)S(1)} %get-tuple-element.21), channel_id=1, source_target_pairs={{0,6},{1,7},{2,8},{3,9},{4,10},{5,11},{6,12},{7,13},{8,14},{9,15},... | collective-permute-start | bytes 196616 | tf_op jit(solution)/shard_map/ppermute | solution.py:68
  291.6 2.2 collective-permute-start.9
  293.7 2.1 collective-permute-start.15
  296.1 2.0 collective-permute-start.17
  298.1 1.3 collective-permute-start.18
  299.4 1.2 collective-permute-start.19
  300.6 1.6 collective-permute-start.20
  302.4 1.5 collective-permute-start.22
  303.9 3.4 %collective-permute-start.8 = (f32[128,128]{1,0:T(8,128)S(1)}, f32[128,128]{1,0:T(8,128)S(1)}, u32[]{:S(2)}, u32[]{:S(2)}) collective-permute-start(f32[128,128]{1,0:T(8,128)S(1)} %get-tuple-element.10), channel_id=1, source_target_pairs={{0,1},{1,2},{2,3},{3,4},{4,5},{5,6},{6,7},{7,8},{8,9},{9,10},{10,1... | collective-permute-start | bytes 196616 | tf_op jit(solution)/shard_map/ppermute | solution.py:68
  307.8 2.2 collective-permute-done.22
  310.0 0.9 add_add_fusion.1
  310.9 1.9 collective-permute-start.23
  312.8 7.6 %collective-permute-done.23 = f32[128,128]{1,0:T(8,128)S(1)} collective-permute-done((f32[128,128]{1,0:T(8,128)S(1)}, f32[128,128]{1,0:T(8,128)S(1)}, u32[]{:S(2)}, u32[]{:S(2)}) %collective-permute-start.23) | collective-permute-done | bytes 65568 | tf_op jit(solution)/shard_map/ppermute | solution.py:106
  (35 shorter events, 3.5 us)
Async XLA Ops:
  0.0 71.8 %collective-permute-start = (f32[3072,128]{1,0:T(8,128)}, f32[3072,128]{1,0:T(8,128)}, u32[]{:S(2)}, u32[]{:S(2)}) collective-permute-start(f32[3072,128]{1,0:T(8,128)} %param.3), channel_id=1, source_target_pairs={{0,16},{16,32},{32,48},{48,0},{1,17},{17,33},{33,49},{49,1},{2,18}... | collective-permute-start | bytes 4718600 | tf_op jit(solution)/shard_map/ppermute | solution.py:59
  3.7 53.5 %collective-permute-start.3 = (f32[512,128]{1,0:T(8,128)S(1)}, f32[512,128]{1,0:T(8,128)S(1)}, u32[]{:S(2)}, u32[]{:S(2)}) collective-permute-start(f32[512,128]{1,0:T(8,128)S(1)} %slice.28), channel_id=1, source_target_pairs={{1,0},{2,1},{3,2},{4,3},{5,4},{6,5},{7,6},{8,7},{9,8},{10,9},{11,1... | collective-permute-start | bytes 786440 | tf_op jit(solution)/shard_map/ppermute | solution.py:13
  57.2 1.9 copy-start
  61.1 5.2 %collective-permute-start.4 = (f32[512,128]{1,0:T(8,128)S(1)}, f32[512,128]{1,0:T(8,128)S(1)}, u32[]{:S(2)}, u32[]{:S(2)}) collective-permute-start(f32[512,128]{1,0:T(8,128)S(1)} %add_bitcast_fusion), channel_id=1, source_target_pairs={{0,1},{1,2},{2,3},{3,4},{4,5},{5,6},{6,7},{7,8},{8,9},{9,10},{10,1... | collective-permute-start | bytes 786440 | tf_op jit(solution)/shard_map/ppermute | solution.py:13
  63.0 69.7 %collective-permute-start.1 = (f32[3072,128]{1,0:T(8,128)S(1)}, f32[3072,128]{1,0:T(8,128)}, u32[]{:S(2)}, u32[]{:S(2)}) collective-permute-start(f32[3072,128]{1,0:T(8,128)S(1)} %copy-done), channel_id=1, source_target_pairs={{0,32},{16,48},{32,0},{48,16},{1,33},{17,49},{33,1},{49,17},{2,34}... | collective-permute-start | bytes 4718600 | tf_op jit(solution)/shard_map/ppermute | solution.py:59
  64.7 100.7 %collective-permute-start.2 = (f32[3072,128]{1,0:T(8,128)S(1)}, f32[3072,128]{1,0:T(8,128)}, u32[]{:S(2)}, u32[]{:S(2)}) collective-permute-start(f32[3072,128]{1,0:T(8,128)S(1)} %copy-done), channel_id=1, source_target_pairs={{0,48},{16,0},{32,16},{48,32},{1,49},{17,1},{33,17},{49,33},{2,50}... | collective-permute-start | bytes 4718600 | tf_op jit(solution)/shard_map/ppermute | solution.py:59
  66.5 133.0 %collective-permute-start.5 = (f32[3072,128]{1,0:T(8,128)S(1)}, f32[3072,128]{1,0:T(8,128)}, u32[]{:S(2)}, u32[]{:S(2)}) collective-permute-start(f32[3072,128]{1,0:T(8,128)S(1)} %bitcast.10), channel_id=1, source_target_pairs={{0,64},{64,128},{128,192},{192,0},{1,65},{65,129},{129,193},{193,1... | collective-permute-start | bytes 4718600 | tf_op jit(solution)/shard_map/ppermute | solution.py:59
  70.7 200.8 %collective-permute-start.6 = (f32[3072,128]{1,0:T(8,128)S(1)}, f32[3072,128]{1,0:T(8,128)}, u32[]{:S(2)}, u32[]{:S(2)}) collective-permute-start(f32[3072,128]{1,0:T(8,128)S(1)} %bitcast.11), channel_id=1, source_target_pairs={{0,128},{64,192},{128,0},{192,64},{1,129},{65,193},{129,1},{193,65... | collective-permute-start | bytes 4718600 | tf_op jit(solution)/shard_map/ppermute | solution.py:59
  71.8 199.8 %collective-permute-start.7 = (f32[3072,128]{1,0:T(8,128)S(1)}, f32[3072,128]{1,0:T(8,128)}, u32[]{:S(2)}, u32[]{:S(2)}) collective-permute-start(f32[3072,128]{1,0:T(8,128)S(1)} %bitcast.12), channel_id=1, source_target_pairs={{0,192},{64,0},{128,64},{192,128},{1,193},{65,1},{129,65},{193,129... | collective-permute-start | bytes 4718600 | tf_op jit(solution)/shard_map/ppermute | solution.py:59
  285.4 6.1 %copy-start.1 = (f32[512,512]{1,0:T(8,128)}, f32[512,512]{1,0:T(8,128)S(1)}, u32[]{:S(2)}) copy-start(f32[512,512]{1,0:T(8,128)S(1)} %fusion) | copy-start | bytes 3145732
  285.5 6.1 %collective-permute-start.10 = (f32[128,128]{1,0:T(8,128)S(1)}, f32[128,128]{1,0:T(8,128)S(1)}, u32[]{:S(2)}, u32[]{:S(2)}) collective-permute-start(f32[128,128]{1,0:T(8,128)S(1)} %get-tuple-element.24), channel_id=1, source_target_pairs={{0,3},{1,4},{2,5},{3,6},{4,7},{5,8},{6,9},{7,10},{8,11},{9,12},{10... | collective-permute-start | bytes 196616 | tf_op jit(solution)/shard_map/ppermute | solution.py:68
  285.8 7.9 %collective-permute-start.11 = (f32[128,128]{1,0:T(8,128)S(1)}, f32[128,128]{1,0:T(8,128)S(1)}, u32[]{:S(2)}, u32[]{:S(2)}) collective-permute-start(f32[128,128]{1,0:T(8,128)S(1)} %get-tuple-element.23), channel_id=1, source_target_pairs={{0,4},{1,5},{2,6},{3,7},{4,8},{5,9},{6,10},{7,11},{8,12},{9,13},{1... | collective-permute-start | bytes 196616 | tf_op jit(solution)/shard_map/ppermute | solution.py:68
  285.9 9.9 %collective-permute-start.12 = (f32[128,128]{1,0:T(8,128)S(1)}, f32[128,128]{1,0:T(8,128)S(1)}, u32[]{:S(2)}, u32[]{:S(2)}) collective-permute-start(f32[128,128]{1,0:T(8,128)S(1)} %get-tuple-element.22), channel_id=1, source_target_pairs={{0,5},{1,6},{2,7},{3,8},{4,9},{5,10},{6,11},{7,12},{8,13},{9,14},{... | collective-permute-start | bytes 196616 | tf_op jit(solution)/shard_map/ppermute | solution.py:68
  286.0 10.1 %collective-permute-start.13 = (f32[128,128]{1,0:T(8,128)S(1)}, f32[128,128]{1,0:T(8,128)S(1)}, u32[]{:S(2)}, u32[]{:S(2)}) collective-permute-start(f32[128,128]{1,0:T(8,128)S(1)} %get-tuple-element.21), channel_id=1, source_target_pairs={{0,6},{1,7},{2,8},{3,9},{4,10},{5,11},{6,12},{7,13},{8,14},{9,15},... | collective-permute-start | bytes 196616 | tf_op jit(solution)/shard_map/ppermute | solution.py:68
  290.9 7.2 %collective-permute-start.14 = (f32[128,128]{1,0:T(8,128)S(1)}, f32[128,128]{1,0:T(8,128)S(1)}, u32[]{:S(2)}, u32[]{:S(2)}) collective-permute-start(f32[128,128]{1,0:T(8,128)S(1)} %get-tuple-element.20), channel_id=1, source_target_pairs={{0,7},{1,8},{2,9},{3,10},{4,11},{5,12},{6,13},{7,14},{8,15},{9,0},... | collective-permute-start | bytes 196616 | tf_op jit(solution)/shard_map/ppermute | solution.py:68
  291.6 7.8 %collective-permute-start.9 = (f32[128,128]{1,0:T(8,128)S(1)}, f32[128,128]{1,0:T(8,128)S(1)}, u32[]{:S(2)}, u32[]{:S(2)}) collective-permute-start(f32[128,128]{1,0:T(8,128)S(1)} %get-tuple-element.19), channel_id=1, source_target_pairs={{0,2},{1,3},{2,4},{3,5},{4,6},{5,7},{6,8},{7,9},{8,10},{9,11},{10,... | collective-permute-start | bytes 196616 | tf_op jit(solution)/shard_map/ppermute | solution.py:68
  293.7 6.8 %collective-permute-start.15 = (f32[128,128]{1,0:T(8,128)S(1)}, f32[128,128]{1,0:T(8,128)S(1)}, u32[]{:S(2)}, u32[]{:S(2)}) collective-permute-start(f32[128,128]{1,0:T(8,128)S(1)} %get-tuple-element.18), channel_id=1, source_target_pairs={{0,8},{1,9},{2,10},{3,11},{4,12},{5,13},{6,14},{7,15},{8,0},{9,1},... | collective-permute-start | bytes 196616 | tf_op jit(solution)/shard_map/ppermute | solution.py:68
  295.8 6.4 %collective-permute-start.16 = (f32[128,128]{1,0:T(8,128)S(1)}, f32[128,128]{1,0:T(8,128)S(1)}, u32[]{:S(2)}, u32[]{:S(2)}) collective-permute-start(f32[128,128]{1,0:T(8,128)S(1)} %get-tuple-element.17), channel_id=1, source_target_pairs={{0,9},{1,10},{2,11},{3,12},{4,13},{5,14},{6,15},{7,0},{8,1},{9,2},... | collective-permute-start | bytes 196616 | tf_op jit(solution)/shard_map/ppermute | solution.py:68
  296.1 6.3 %collective-permute-start.17 = (f32[128,128]{1,0:T(8,128)S(1)}, f32[128,128]{1,0:T(8,128)S(1)}, u32[]{:S(2)}, u32[]{:S(2)}) collective-permute-start(f32[128,128]{1,0:T(8,128)S(1)} %get-tuple-element.16), channel_id=1, source_target_pairs={{0,10},{1,11},{2,12},{3,13},{4,14},{5,15},{6,0},{7,1},{8,2},{9,3},... | collective-permute-start | bytes 196616 | tf_op jit(solution)/shard_map/ppermute | solution.py:68
  298.1 5.9 %collective-permute-start.18 = (f32[128,128]{1,0:T(8,128)S(1)}, f32[128,128]{1,0:T(8,128)S(1)}, u32[]{:S(2)}, u32[]{:S(2)}) collective-permute-start(f32[128,128]{1,0:T(8,128)S(1)} %get-tuple-element.15), channel_id=1, source_target_pairs={{0,11},{1,12},{2,13},{3,14},{4,15},{5,0},{6,1},{7,2},{8,3},{9,4},{... | collective-permute-start | bytes 196616 | tf_op jit(solution)/shard_map/ppermute | solution.py:68
  299.4 8.0 %collective-permute-start.19 = (f32[128,128]{1,0:T(8,128)S(1)}, f32[128,128]{1,0:T(8,128)S(1)}, u32[]{:S(2)}, u32[]{:S(2)}) collective-permute-start(f32[128,128]{1,0:T(8,128)S(1)} %get-tuple-element.14), channel_id=1, source_target_pairs={{0,12},{1,13},{2,14},{3,15},{4,0},{5,1},{6,2},{7,3},{8,4},{9,5},{1... | collective-permute-start | bytes 196616 | tf_op jit(solution)/shard_map/ppermute | solution.py:68
  300.6 6.8 %collective-permute-start.20 = (f32[128,128]{1,0:T(8,128)S(1)}, f32[128,128]{1,0:T(8,128)S(1)}, u32[]{:S(2)}, u32[]{:S(2)}) collective-permute-start(f32[128,128]{1,0:T(8,128)S(1)} %get-tuple-element.13), channel_id=1, source_target_pairs={{0,13},{1,14},{2,15},{3,0},{4,1},{5,2},{6,3},{7,4},{8,5},{9,6},{10... | collective-permute-start | bytes 196616 | tf_op jit(solution)/shard_map/ppermute | solution.py:68
  302.2 5.6 %collective-permute-start.21 = (f32[128,128]{1,0:T(8,128)S(1)}, f32[128,128]{1,0:T(8,128)S(1)}, u32[]{:S(2)}, u32[]{:S(2)}) collective-permute-start(f32[128,128]{1,0:T(8,128)S(1)} %get-tuple-element.12), channel_id=1, source_target_pairs={{0,14},{1,15},{2,0},{3,1},{4,2},{5,3},{6,4},{7,5},{8,6},{9,7},{10,... | collective-permute-start | bytes 196616 | tf_op jit(solution)/shard_map/ppermute | solution.py:68
  302.4 7.5 %collective-permute-start.22 = (f32[128,128]{1,0:T(8,128)S(1)}, f32[128,128]{1,0:T(8,128)S(1)}, u32[]{:S(2)}, u32[]{:S(2)}) collective-permute-start(f32[128,128]{1,0:T(8,128)S(1)} %get-tuple-element.11), channel_id=1, source_target_pairs={{0,15},{1,0},{2,1},{3,2},{4,3},{5,4},{6,5},{7,6},{8,7},{9,8},{10,9... | collective-permute-start | bytes 196616 | tf_op jit(solution)/shard_map/ppermute | solution.py:68
  303.9 6.0 %collective-permute-start.8 = (f32[128,128]{1,0:T(8,128)S(1)}, f32[128,128]{1,0:T(8,128)S(1)}, u32[]{:S(2)}, u32[]{:S(2)}) collective-permute-start(f32[128,128]{1,0:T(8,128)S(1)} %get-tuple-element.10), channel_id=1, source_target_pairs={{0,1},{1,2},{2,3},{3,4},{4,5},{5,6},{6,7},{7,8},{8,9},{9,10},{10,1... | collective-permute-start | bytes 196616 | tf_op jit(solution)/shard_map/ppermute | solution.py:68
  310.9 9.5 %collective-permute-start.23 = (f32[128,128]{1,0:T(8,128)S(1)}, f32[128,128]{1,0:T(8,128)S(1)}, u32[]{:S(2)}, u32[]{:S(2)}) collective-permute-start(f32[128,128]{1,0:T(8,128)S(1)} %add_add_fusion.1), channel_id=1, source_target_pairs={{0,0},{1,4},{2,8},{3,12},{4,16},{5,20},{6,24},{7,28},{8,32},{9,36}... | collective-permute-start | bytes 196616 | tf_op jit(solution)/shard_map/ppermute | solution.py:106

commit v3 on v2

--- a/solution.py
+++ b/solution.py
@@ -47,7 +47,7 @@
         left,
         right,
         (((0,), (0,)), ((), ())),
-        precision=lax.Precision.HIGHEST,
+        precision=lax.Precision.HIGH,
         preferred_element_type=jnp.float32,
     )
 
@@ -58,17 +58,6 @@
     for shift in range(1, count):
         held.append(lax.ppermute(block, axis, [(i, (i + shift) % count) for i in range(count)]))
     return jnp.concatenate(held, 1)
-
-
-def direct_reduce_scatter(piece_of, axis):
-    count = lax.axis_size(axis)
-    me = lax.axis_index(axis)
-    total = piece_of(me)
-    for shift in range(1, count):
-        total = total + lax.ppermute(
-            piece_of((me + shift) % count), axis, [(i, (i + shift) % count) for i in range(count)]
-        )
-    return total
 
 
 def local(snapshots, region_ids, conductivity):
@@ -88,22 +77,24 @@
     rows = ring_gather(snapshots, "c")
     cols = ring_gather(panel, "r")
     partial_value = contract(rows, cols)
-    me_r, me_c = lax.axis_index("r"), lax.axis_index("c")
+    me_r, me_c, me_t = lax.axis_index("r"), lax.axis_index("c"), lax.axis_index("mesh")
 
-    def piece_of(t):
-        row_block = (me_c - t // side) % side
-        col_block = (me_r - t % side) % side
+    def piece_of(j):
+        row_block = (me_c - j // side) % side
+        col_block = (me_r - j % side) % side
         return lax.dynamic_slice(
             partial_value, (row_block * group_cols, col_block * group_cols), (group_cols, group_cols)
         )
 
-    summed = direct_reduce_scatter(piece_of, "mesh")
-    perm = []
-    for c in range(side):
-        for t in range(tiles):
-            dest_c, dest_t = t // side, c + side * (t % side)
-            perm.append((c * tiles + t, dest_c * tiles + dest_t))
-    placed = lax.ppermute(summed, ("c", "mesh"), perm)
+    placed = None
+    for step in range(tiles):
+        perm = []
+        for c in range(side):
+            for t in range(tiles):
+                j = (t + step) % tiles
+                perm.append((c * tiles + t, (j // side) * tiles + c + side * (j % side)))
+        moved = lax.ppermute(piece_of((me_t + step) % tiles), ("c", "mesh"), perm)
+        placed = moved if placed is None else placed + moved
     total_nodes = node_rows * tiles
     return placed / math.sqrt(total_nodes)
 

time: 321 us -> 334 us (1.040)
  the two profiles are of different devices: /device:TPU:89 before, /device:TPU:113 now
where the time goes in v3:
time: 334 us
  waiting for transfers between devices  212 us (63%)
  starting transfers between devices  103 us (31%)
  matrix products  8.79 us (3%)
  other arithmetic  5.55 us (2%)
  local copies, waits for them, and re-layouts  3.48 us (1%)
    ppermute x6, waiting for transfers between devices, ring_gather(): lax.ppermute(block, axis, [(i, (i + shift) % count) for i in range(count)])  199 us
    ppermute x16, starting transfers between devices, local(): moved = lax.ppermute(piece_of((me_t + step) % tiles), ('c', 'mesh'), perm)  89.8 us
    dot_general x1, matrix products, contract(): lax.dot_general(left, right, (((0,), (0,)), ((), ())), precision=lax.Prec...  8.79 us
    ppermute x6, starting transfers between devices, ring_gather(): lax.ppermute(block, axis, [(i, (i + shift) % count) for i in range(count)])  8.43 us
    ppermute x16, waiting for transfers between devices, local(): moved = lax.ppermute(piece_of((me_t + step) % tiles), ('c', 'mesh'), perm)  7.23 us
  transfers between devices with their start and end apart: 24, of which 10 were waited for; matrix products, arithmetic and copies ran while one was open for 2% of the time, Pallas kernels for 0%

profile of v3, /device:TPU:113, one launch (start us, length us, event | category | flops | bytes accessed | tf_op | source)
XLA Modules:
  0.0 334.0 jit_solution(14775128635862791305)
XLA Ops:
  0.0 2.7 collective-permute-start
  3.7 2.9 collective-permute-start.3
  7.5 4.5 %collective-permute-done.3 = f32[512,128]{1,0:T(8,128)S(1)} collective-permute-done((f32[512,128]{1,0:T(8,128)S(1)}, f32[512,128]{1,0:T(8,128)S(1)}, u32[]{:S(2)}, u32[]{:S(2)}) %collective-permute-start.3) | collective-permute-done | bytes 262176 | tf_op jit(solution)/shard_map/ppermute | solution.py:13
  12.0 1.6 pad_maximum_fusion
  14.5 1.3 add_multiply_fusion.2
  15.8 1.9 collective-permute-start.4
  17.8 1.2 collective-permute-start.2
  19.3 1.7 collective-permute-done.4
  21.2 3.4 %collective-permute-start.5 = (f32[3072,128]{1,0:T(8,128)S(1)}, f32[3072,128]{1,0:T(8,128)}, u32[]{:S(2)}, u32[]{:S(2)}) collective-permute-start(f32[3072,128]{1,0:T(8,128)S(1)} %bitcast.10), channel_id=1, source_target_pairs={{0,64},{64,128},{128,192},{192,0},{1,65},{65,129},{129,193},{193,1... | collective-permute-start | bytes 4718600 | tf_op jit(solution)/shard_map/ppermute | solution.py:59
  24.5 1.0 collective-permute-start.6
  25.6 46.2 %collective-permute-done = f32[3072,128]{1,0:T(8,128)} collective-permute-done((f32[3072,128]{1,0:T(8,128)}, f32[3072,128]{1,0:T(8,128)}, u32[]{:S(2)}, u32[]{:S(2)}) %collective-permute-start) | collective-permute-done | bytes 1572896 | tf_op jit(solution)/shard_map/ppermute | solution.py:59
  71.7 15.3 %collective-permute-done.1 = f32[3072,128]{1,0:T(8,128)} collective-permute-done((f32[3072,128]{1,0:T(8,128)S(1)}, f32[3072,128]{1,0:T(8,128)}, u32[]{:S(2)}, u32[]{:S(2)}) %collective-permute-start.1) | collective-permute-done | bytes 1572896 | tf_op jit(solution)/shard_map/ppermute | solution.py:59
  87.1 31.6 %collective-permute-done.2 = f32[3072,128]{1,0:T(8,128)} collective-permute-done((f32[3072,128]{1,0:T(8,128)S(1)}, f32[3072,128]{1,0:T(8,128)}, u32[]{:S(2)}, u32[]{:S(2)}) %collective-permute-start.2) | collective-permute-done | bytes 1572896 | tf_op jit(solution)/shard_map/ppermute | solution.py:59
  118.7 73.0 %collective-permute-done.6 = f32[3072,128]{1,0:T(8,128)} collective-permute-done((f32[3072,128]{1,0:T(8,128)S(1)}, f32[3072,128]{1,0:T(8,128)}, u32[]{:S(2)}, u32[]{:S(2)}) %collective-permute-start.6) | collective-permute-done | bytes 1572896 | tf_op jit(solution)/shard_map/ppermute | solution.py:59
  191.6 32.8 %collective-permute-done.7 = f32[3072,128]{1,0:T(8,128)} collective-permute-done((f32[3072,128]{1,0:T(8,128)S(1)}, f32[3072,128]{1,0:T(8,128)}, u32[]{:S(2)}, u32[]{:S(2)}) %collective-permute-start.7) | collective-permute-done | bytes 1572896 | tf_op jit(solution)/shard_map/ppermute | solution.py:59
  224.4 8.8 %fusion = f32[512,512]{1,0:T(8,128)S(1)} fusion(f32[3072,128]{1,0:T(8,128)} %collective-permute-done.2, f32[3072,128]{1,0:T(8,128)} %collective-permute-done.1, f32[3072,128]{1,0:T(8,128)} %collective-permute-done, f32[3072,128]{1,0:T(8,128)S(1)} %copy-done, f32[3072,128]{1,0:T(8,128)} %collective-permute-done.7, f32[3072,128]{1,0:T(8,128)} %collective-permute-done.6, ...), kind=kOutput, calls=%fused_computation | convolution fusion | flops 4841275392 | bytes 13631488 | tf_op jit(solution)/shard_map/dot_general | solution.py:46
  235.3 3.6 %collective-permute-start.11 = (f32[128,128]{1,0:T(8,128)S(1)}, f32[128,128]{1,0:T(8,128)S(1)}, u32[]{:S(2)}, u32[]{:S(2)}) collective-permute-start(f32[128,128]{1,0:T(8,128)S(1)} %get-tuple-element.24), channel_id=1, source_target_pairs={{0,12},{1,16},{2,20},{3,24},{4,28},{5,32},{6,36},{7,40},{8,44},{9,... | collective-permute-start | bytes 196616 | tf_op jit(solution)/shard_map/ppermute | solution.py:96
  238.9 44.7 %collective-permute-start.12 = (f32[128,128]{1,0:T(8,128)S(1)}, f32[128,128]{1,0:T(8,128)S(1)}, u32[]{:S(2)}, u32[]{:S(2)}) collective-permute-start(f32[128,128]{1,0:T(8,128)S(1)} %get-tuple-element.23), channel_id=1, source_target_pairs={{0,16},{1,20},{2,24},{3,28},{4,32},{5,36},{6,40},{7,44},{8,48},{9,... | collective-permute-start | bytes 196616 | tf_op jit(solution)/shard_map/ppermute | solution.py:96
  283.6 4.3 %collective-permute-start.13 = (f32[128,128]{1,0:T(8,128)S(1)}, f32[128,128]{1,0:T(8,128)S(1)}, u32[]{:S(2)}, u32[]{:S(2)}) collective-permute-start(f32[128,128]{1,0:T(8,128)S(1)} %get-tuple-element.22), channel_id=1, source_target_pairs={{0,20},{1,24},{2,28},{3,32},{4,36},{5,40},{6,44},{7,48},{8,52},{9,... | collective-permute-start | bytes 196616 | tf_op jit(solution)/shard_map/ppermute | solution.py:96
  287.9 1.9 collective-permute-start.14
  289.8 1.9 collective-permute-start.15
  291.7 1.2 fusion.18
  292.9 7.3 %collective-permute-start.8 = (f32[128,128]{1,0:T(8,128)S(1)}, f32[128,128]{1,0:T(8,128)S(1)}, u32[]{:S(2)}, u32[]{:S(2)}) collective-permute-start(f32[128,128]{1,0:T(8,128)S(1)} %get-tuple-element.19), channel_id=1, source_target_pairs={{0,0},{1,4},{2,8},{3,12},{4,16},{5,20},{6,24},{7,28},{8,32},{9,36}... | collective-permute-start | bytes 196616 | tf_op jit(solution)/shard_map/ppermute | solution.py:96
  300.2 4.7 %collective-permute-start.16 = (f32[128,128]{1,0:T(8,128)S(1)}, f32[128,128]{1,0:T(8,128)S(1)}, u32[]{:S(2)}, u32[]{:S(2)}) collective-permute-start(f32[128,128]{1,0:T(8,128)S(1)} %get-tuple-element.18), channel_id=1, source_target_pairs={{0,32},{1,36},{2,40},{3,44},{4,48},{5,52},{6,56},{7,60},{8,0},{9,4... | collective-permute-start | bytes 196616 | tf_op jit(solution)/shard_map/ppermute | solution.py:96
  304.9 2.0 collective-permute-start.17
  307.0 3.2 collective-permute-start.18
  310.1 4.2 %collective-permute-start.19 = (f32[128,128]{1,0:T(8,128)S(1)}, f32[128,128]{1,0:T(8,128)S(1)}, u32[]{:S(2)}, u32[]{:S(2)}) collective-permute-start(f32[128,128]{1,0:T(8,128)S(1)} %get-tuple-element.15), channel_id=1, source_target_pairs={{0,44},{1,48},{2,52},{3,56},{4,60},{5,0},{6,4},{7,8},{8,12},{9,16}... | collective-permute-start | bytes 196616 | tf_op jit(solution)/shard_map/ppermute | solution.py:96
  314.5 5.0 %collective-permute-start.21 = (f32[128,128]{1,0:T(8,128)S(1)}, f32[128,128]{1,0:T(8,128)S(1)}, u32[]{:S(2)}, u32[]{:S(2)}) collective-permute-start(f32[128,128]{1,0:T(8,128)S(1)} %get-tuple-element.13), channel_id=1, source_target_pairs={{0,52},{1,56},{2,60},{3,0},{4,4},{5,8},{6,12},{7,16},{8,20},{9,24}... | collective-permute-start | bytes 196616 | tf_op jit(solution)/shard_map/ppermute | solution.py:96
  319.5 1.9 collective-permute-start.22
  321.4 3.8 %collective-permute-start.23 = (f32[128,128]{1,0:T(8,128)S(1)}, f32[128,128]{1,0:T(8,128)S(1)}, u32[]{:S(2)}, u32[]{:S(2)}) collective-permute-start(f32[128,128]{1,0:T(8,128)S(1)} %get-tuple-element.11), channel_id=1, source_target_pairs={{0,60},{1,0},{2,4},{3,8},{4,12},{5,16},{6,20},{7,24},{8,28},{9,32}... | collective-permute-start | bytes 196616 | tf_op jit(solution)/shard_map/ppermute | solution.py:96
  326.3 2.6 collective-permute-done.23
  328.8 4.5 %collective-permute-done.9 = f32[128,128]{1,0:T(8,128)S(1)} collective-permute-done((f32[128,128]{1,0:T(8,128)S(1)}, f32[128,128]{1,0:T(8,128)S(1)}, u32[]{:S(2)}, u32[]{:S(2)}) %collective-permute-start.9) | collective-permute-done | bytes 65568 | tf_op jit(solution)/shard_map/ppermute | solution.py:96
  (34 shorter events, 6.6 us)
Async XLA Ops:
  0.0 71.7 %collective-permute-start = (f32[3072,128]{1,0:T(8,128)}, f32[3072,128]{1,0:T(8,128)}, u32[]{:S(2)}, u32[]{:S(2)}) collective-permute-start(f32[3072,128]{1,0:T(8,128)} %param.3), channel_id=1, source_target_pairs={{0,16},{16,32},{32,48},{48,0},{1,17},{17,33},{33,49},{49,1},{2,18}... | collective-permute-start | bytes 4718600 | tf_op jit(solution)/shard_map/ppermute | solution.py:59
  3.7 8.2 %collective-permute-start.3 = (f32[512,128]{1,0:T(8,128)S(1)}, f32[512,128]{1,0:T(8,128)S(1)}, u32[]{:S(2)}, u32[]{:S(2)}) collective-permute-start(f32[512,128]{1,0:T(8,128)S(1)} %slice.28), channel_id=1, source_target_pairs={{1,0},{2,1},{3,2},{4,3},{5,4},{6,5},{7,6},{8,7},{9,8},{10,9},{11,1... | collective-permute-start | bytes 786440 | tf_op jit(solution)/shard_map/ppermute | solution.py:13
  11.9 1.9 copy-start
  15.8 5.2 %collective-permute-start.4 = (f32[512,128]{1,0:T(8,128)S(1)}, f32[512,128]{1,0:T(8,128)S(1)}, u32[]{:S(2)}, u32[]{:S(2)}) collective-permute-start(f32[512,128]{1,0:T(8,128)S(1)} %add_bitcast_fusion), channel_id=1, source_target_pairs={{0,1},{1,2},{2,3},{3,4},{4,5},{5,6},{6,7},{7,8},{8,9},{9,10},{10,1... | collective-permute-start | bytes 786440 | tf_op jit(solution)/shard_map/ppermute | solution.py:13
  17.7 69.4 %collective-permute-start.1 = (f32[3072,128]{1,0:T(8,128)S(1)}, f32[3072,128]{1,0:T(8,128)}, u32[]{:S(2)}, u32[]{:S(2)}) collective-permute-start(f32[3072,128]{1,0:T(8,128)S(1)} %copy-done), channel_id=1, source_target_pairs={{0,32},{16,48},{32,0},{48,16},{1,33},{17,49},{33,1},{49,17},{2,34}... | collective-permute-start | bytes 4718600 | tf_op jit(solution)/shard_map/ppermute | solution.py:59
  17.8 100.9 %collective-permute-start.2 = (f32[3072,128]{1,0:T(8,128)S(1)}, f32[3072,128]{1,0:T(8,128)}, u32[]{:S(2)}, u32[]{:S(2)}) collective-permute-start(f32[3072,128]{1,0:T(8,128)S(1)} %copy-done), channel_id=1, source_target_pairs={{0,48},{16,0},{32,16},{48,32},{1,49},{17,1},{33,17},{49,33},{2,50}... | collective-permute-start | bytes 4718600 | tf_op jit(solution)/shard_map/ppermute | solution.py:59
  21.2 97.5 %collective-permute-start.5 = (f32[3072,128]{1,0:T(8,128)S(1)}, f32[3072,128]{1,0:T(8,128)}, u32[]{:S(2)}, u32[]{:S(2)}) collective-permute-start(f32[3072,128]{1,0:T(8,128)S(1)} %bitcast.10), channel_id=1, source_target_pairs={{0,64},{64,128},{128,192},{192,0},{1,65},{65,129},{129,193},{193,1... | collective-permute-start | bytes 4718600 | tf_op jit(solution)/shard_map/ppermute | solution.py:59
  24.5 167.1 %collective-permute-start.6 = (f32[3072,128]{1,0:T(8,128)S(1)}, f32[3072,128]{1,0:T(8,128)}, u32[]{:S(2)}, u32[]{:S(2)}) collective-permute-start(f32[3072,128]{1,0:T(8,128)S(1)} %bitcast.11), channel_id=1, source_target_pairs={{0,128},{64,192},{128,0},{192,64},{1,129},{65,193},{129,1},{193,65... | collective-permute-start | bytes 4718600 | tf_op jit(solution)/shard_map/ppermute | solution.py:59
  71.7 152.7 %collective-permute-start.7 = (f32[3072,128]{1,0:T(8,128)S(1)}, f32[3072,128]{1,0:T(8,128)}, u32[]{:S(2)}, u32[]{:S(2)}) collective-permute-start(f32[3072,128]{1,0:T(8,128)S(1)} %bitcast.12), channel_id=1, source_target_pairs={{0,192},{64,0},{128,64},{192,128},{1,193},{65,1},{129,65},{193,129... | collective-permute-start | bytes 4718600 | tf_op jit(solution)/shard_map/ppermute | solution.py:59
  233.2 1.0 copy-start.1
  234.3 55.5 %collective-permute-start.10 = (f32[128,128]{1,0:T(8,128)S(1)}, f32[128,128]{1,0:T(8,128)S(1)}, u32[]{:S(2)}, u32[]{:S(2)}) collective-permute-start(f32[128,128]{1,0:T(8,128)S(1)} %get-tuple-element.25), channel_id=1, source_target_pairs={{0,8},{1,12},{2,16},{3,20},{4,24},{5,28},{6,32},{7,36},{8,40},{9,4... | collective-permute-start | bytes 196616 | tf_op jit(solution)/shard_map/ppermute | solution.py:96
  235.3 57.6 %collective-permute-start.11 = (f32[128,128]{1,0:T(8,128)S(1)}, f32[128,128]{1,0:T(8,128)S(1)}, u32[]{:S(2)}, u32[]{:S(2)}) collective-permute-start(f32[128,128]{1,0:T(8,128)S(1)} %get-tuple-element.24), channel_id=1, source_target_pairs={{0,12},{1,16},{2,20},{3,24},{4,28},{5,32},{6,36},{7,40},{8,44},{9,... | collective-permute-start | bytes 196616 | tf_op jit(solution)/shard_map/ppermute | solution.py:96
  238.9 61.3 %collective-permute-start.12 = (f32[128,128]{1,0:T(8,128)S(1)}, f32[128,128]{1,0:T(8,128)S(1)}, u32[]{:S(2)}, u32[]{:S(2)}) collective-permute-start(f32[128,128]{1,0:T(8,128)S(1)} %get-tuple-element.23), channel_id=1, source_target_pairs={{0,16},{1,20},{2,24},{3,28},{4,32},{5,36},{6,40},{7,44},{8,48},{9,... | collective-permute-start | bytes 196616 | tf_op jit(solution)/shard_map/ppermute | solution.py:96
  283.6 21.3 %collective-permute-start.13 = (f32[128,128]{1,0:T(8,128)S(1)}, f32[128,128]{1,0:T(8,128)S(1)}, u32[]{:S(2)}, u32[]{:S(2)}) collective-permute-start(f32[128,128]{1,0:T(8,128)S(1)} %get-tuple-element.22), channel_id=1, source_target_pairs={{0,20},{1,24},{2,28},{3,32},{4,36},{5,40},{6,44},{7,48},{8,52},{9,... | collective-permute-start | bytes 196616 | tf_op jit(solution)/shard_map/ppermute | solution.py:96
  287.9 19.1 %collective-permute-start.14 = (f32[128,128]{1,0:T(8,128)S(1)}, f32[128,128]{1,0:T(8,128)S(1)}, u32[]{:S(2)}, u32[]{:S(2)}) collective-permute-start(f32[128,128]{1,0:T(8,128)S(1)} %get-tuple-element.21), channel_id=1, source_target_pairs={{0,24},{1,28},{2,32},{3,36},{4,40},{5,44},{6,48},{7,52},{8,56},{9,... | collective-permute-start | bytes 196616 | tf_op jit(solution)/shard_map/ppermute | solution.py:96
  289.8 20.3 %collective-permute-start.15 = (f32[128,128]{1,0:T(8,128)S(1)}, f32[128,128]{1,0:T(8,128)S(1)}, u32[]{:S(2)}, u32[]{:S(2)}) collective-permute-start(f32[128,128]{1,0:T(8,128)S(1)} %get-tuple-element.20), channel_id=1, source_target_pairs={{0,28},{1,32},{2,36},{3,40},{4,44},{5,48},{6,52},{7,56},{8,60},{9,... | collective-permute-start | bytes 196616 | tf_op jit(solution)/shard_map/ppermute | solution.py:96
  292.9 21.4 %collective-permute-start.8 = (f32[128,128]{1,0:T(8,128)S(1)}, f32[128,128]{1,0:T(8,128)S(1)}, u32[]{:S(2)}, u32[]{:S(2)}) collective-permute-start(f32[128,128]{1,0:T(8,128)S(1)} %get-tuple-element.19), channel_id=1, source_target_pairs={{0,0},{1,4},{2,8},{3,12},{4,16},{5,20},{6,24},{7,28},{8,32},{9,36}... | collective-permute-start | bytes 196616 | tf_op jit(solution)/shard_map/ppermute | solution.py:96
  300.2 14.2 %collective-permute-start.16 = (f32[128,128]{1,0:T(8,128)S(1)}, f32[128,128]{1,0:T(8,128)S(1)}, u32[]{:S(2)}, u32[]{:S(2)}) collective-permute-start(f32[128,128]{1,0:T(8,128)S(1)} %get-tuple-element.18), channel_id=1, source_target_pairs={{0,32},{1,36},{2,40},{3,44},{4,48},{5,52},{6,56},{7,60},{8,0},{9,4... | collective-permute-start | bytes 196616 | tf_op jit(solution)/shard_map/ppermute | solution.py:96
  304.9 14.6 %collective-permute-start.17 = (f32[128,128]{1,0:T(8,128)S(1)}, f32[128,128]{1,0:T(8,128)S(1)}, u32[]{:S(2)}, u32[]{:S(2)}) collective-permute-start(f32[128,128]{1,0:T(8,128)S(1)} %get-tuple-element.17), channel_id=1, source_target_pairs={{0,36},{1,40},{2,44},{3,48},{4,52},{5,56},{6,60},{7,0},{8,4},{9,8}... | collective-permute-start | bytes 196616 | tf_op jit(solution)/shard_map/ppermute | solution.py:96
  307.0 14.4 %collective-permute-start.18 = (f32[128,128]{1,0:T(8,128)S(1)}, f32[128,128]{1,0:T(8,128)S(1)}, u32[]{:S(2)}, u32[]{:S(2)}) collective-permute-start(f32[128,128]{1,0:T(8,128)S(1)} %get-tuple-element.16), channel_id=1, source_target_pairs={{0,40},{1,44},{2,48},{3,52},{4,56},{5,60},{6,0},{7,4},{8,8},{9,12}... | collective-permute-start | bytes 196616 | tf_op jit(solution)/shard_map/ppermute | solution.py:96
  310.1 15.0 %collective-permute-start.19 = (f32[128,128]{1,0:T(8,128)S(1)}, f32[128,128]{1,0:T(8,128)S(1)}, u32[]{:S(2)}, u32[]{:S(2)}) collective-permute-start(f32[128,128]{1,0:T(8,128)S(1)} %get-tuple-element.15), channel_id=1, source_target_pairs={{0,44},{1,48},{2,52},{3,56},{4,60},{5,0},{6,4},{7,8},{8,12},{9,16}... | collective-permute-start | bytes 196616 | tf_op jit(solution)/shard_map/ppermute | solution.py:96
  314.3 11.8 %collective-permute-start.20 = (f32[128,128]{1,0:T(8,128)S(1)}, f32[128,128]{1,0:T(8,128)S(1)}, u32[]{:S(2)}, u32[]{:S(2)}) collective-permute-start(f32[128,128]{1,0:T(8,128)S(1)} %get-tuple-element.14), channel_id=1, source_target_pairs={{0,48},{1,52},{2,56},{3,60},{4,0},{5,4},{6,8},{7,12},{8,16},{9,20}... | collective-permute-start | bytes 196616 | tf_op jit(solution)/shard_map/ppermute | solution.py:96
  314.5 11.7 %collective-permute-start.21 = (f32[128,128]{1,0:T(8,128)S(1)}, f32[128,128]{1,0:T(8,128)S(1)}, u32[]{:S(2)}, u32[]{:S(2)}) collective-permute-start(f32[128,128]{1,0:T(8,128)S(1)} %get-tuple-element.13), channel_id=1, source_target_pairs={{0,52},{1,56},{2,60},{3,0},{4,4},{5,8},{6,12},{7,16},{8,20},{9,24}... | collective-permute-start | bytes 196616 | tf_op jit(solution)/shard_map/ppermute | solution.py:96
  319.5 6.8 %collective-permute-start.22 = (f32[128,128]{1,0:T(8,128)S(1)}, f32[128,128]{1,0:T(8,128)S(1)}, u32[]{:S(2)}, u32[]{:S(2)}) collective-permute-start(f32[128,128]{1,0:T(8,128)S(1)} %get-tuple-element.12), channel_id=1, source_target_pairs={{0,56},{1,60},{2,0},{3,4},{4,8},{5,12},{6,16},{7,20},{8,24},{9,28}... | collective-permute-start | bytes 196616 | tf_op jit(solution)/shard_map/ppermute | solution.py:96
  321.4 7.5 %collective-permute-start.23 = (f32[128,128]{1,0:T(8,128)S(1)}, f32[128,128]{1,0:T(8,128)S(1)}, u32[]{:S(2)}, u32[]{:S(2)}) collective-permute-start(f32[128,128]{1,0:T(8,128)S(1)} %get-tuple-element.11), channel_id=1, source_target_pairs={{0,60},{1,0},{2,4},{3,8},{4,12},{5,16},{6,20},{7,24},{8,28},{9,32}... | collective-permute-start | bytes 196616 | tf_op jit(solution)/shard_map/ppermute | solution.py:96
  325.1 8.2 %collective-permute-start.9 = (f32[128,128]{1,0:T(8,128)S(1)}, f32[128,128]{1,0:T(8,128)S(1)}, u32[]{:S(2)}, u32[]{:S(2)}) collective-permute-start(f32[128,128]{1,0:T(8,128)S(1)} %get-tuple-element.10), channel_id=1, source_target_pairs={{0,4},{1,8},{2,12},{3,16},{4,20},{5,24},{6,28},{7,32},{8,36},{9,40... | collective-permute-start | bytes 196616 | tf_op jit(solution)/shard_map/ppermute | solution.py:96

commit v4 on v3

--- a/solution.py
+++ b/solution.py
@@ -52,12 +52,36 @@
     )
 
 
+def pairs(count, to):
+    return [(i, to(i)) for i in range(count)]
+
+
+def square_gather(block, axis):
+    count, half = lax.axis_size(axis), block.shape[0] // 2
+    from_x = lax.ppermute(block, axis, pairs(count, lambda i: i ^ 1))
+    from_z = lax.ppermute(block, axis, pairs(count, lambda i: i ^ 2))
+    corner = jnp.concatenate(
+        [
+            lax.ppermute(from_x[:half], axis, pairs(count, lambda i: i ^ 2)),
+            lax.ppermute(from_z[half:], axis, pairs(count, lambda i: i ^ 1)),
+        ],
+        0,
+    )
+    return jnp.concatenate([block, from_x, from_z, corner], 1)
+
+
 def ring_gather(block, axis):
-    count = lax.axis_size(axis)
-    held = [block]
-    for shift in range(1, count):
-        held.append(lax.ppermute(block, axis, [(i, (i + shift) % count) for i in range(count)]))
-    return jnp.concatenate(held, 1)
+    count, half = lax.axis_size(axis), block.shape[0] // 2
+    from_left = lax.ppermute(block, axis, pairs(count, lambda i: (i + 1) % count))
+    from_right = lax.ppermute(block, axis, pairs(count, lambda i: (i - 1) % count))
+    far = jnp.concatenate(
+        [
+            lax.ppermute(from_left[:half], axis, pairs(count, lambda i: (i + 1) % count)),
+            lax.ppermute(from_right[half:], axis, pairs(count, lambda i: (i - 1) % count)),
+        ],
+        0,
+    )
+    return jnp.concatenate([block, from_left, far, from_right], 1)
 
 
 def local(snapshots, region_ids, conductivity):
@@ -74,13 +98,13 @@
     panel = jnp.concatenate([inner[:1] + carried[None], inner[1:]], 0).reshape(
         node_rows, group_cols
     )
-    rows = ring_gather(snapshots, "c")
+    rows = square_gather(snapshots, "c")
     cols = ring_gather(panel, "r")
     partial_value = contract(rows, cols)
     me_r, me_c, me_t = lax.axis_index("r"), lax.axis_index("c"), lax.axis_index("mesh")
 
     def piece_of(j):
-        row_block = (me_c - j // side) % side
+        row_block = jnp.bitwise_xor(me_c, j // side)
         col_block = (me_r - j % side) % side
         return lax.dynamic_slice(
             partial_value, (row_block * group_cols, col_block * group_cols), (group_cols, group_cols)

time: 334 us -> 244 us (0.73)
  the two profiles are of different devices: /device:TPU:113 before, /device:TPU:22 now
where the time goes in v4:
time: 244 us; the launch traced here: 243 us
  waiting for transfers between devices  150 us (61%)
  starting transfers between devices  71 us (29%)
  matrix products  8.8 us (4%)
  local copies, waits for them, and re-layouts  7.52 us (3%)
  other arithmetic  5.55 us (2%)
    ppermute x1, waiting for transfers between devices, ring_gather(): lax.ppermute(block, axis, pairs(count, lambda i: (i + 1) % count))  52.8 us
    ppermute x16, starting transfers between devices, local(): moved = lax.ppermute(piece_of((me_t + step) % tiles), ('c', 'mesh'), perm)  47.5 us
    ppermute x1, waiting for transfers between devices, square_gather(): from_z = lax.ppermute(block, axis, pairs(count, lambda i: i ^ 2))  31.6 us
    ppermute x1, waiting for transfers between devices, square_gather(): from_x = lax.ppermute(block, axis, pairs(count, lambda i: i ^ 1))  27.1 us
    ppermute x1, waiting for transfers between devices, ring_gather(): lax.ppermute(from_left[:half], axis, pairs(count, lambda i: (i + 1) % cou...  21.4 us
    dot_general x1, matrix products, contract(): lax.dot_general(left, right, (((0,), (0,)), ((), ())), precision=lax.Prec...  8.8 us
    ppermute x16, waiting for transfers between devices, local(): moved = lax.ppermute(piece_of((me_t + step) % tiles), ('c', 'mesh'), perm)  8.18 us
    ppermute x2, starting transfers between devices, passed_along(): lax.ppermute(value, axis, [(source, source + steps) for source in range(f...  5.56 us
  transfers between devices with their start and end apart: 26, of which 9 were waited for; matrix products, arithmetic and copies ran while one was open for 3% of the time, Pallas kernels for 0%

profile of v4, /device:TPU:22, one launch (start us, length us, event | category | flops | bytes accessed | tf_op | source)
XLA Modules:
  0.0 243.3 jit_solution(10786676860920688433)
XLA Ops:
  1.0 1.9 collective-permute-start.4
  3.7 3.0 %collective-permute-done.4 = f32[512,128]{1,0:T(8,128)S(1)} collective-permute-done((f32[512,128]{1,0:T(8,128)S(1)}, f32[512,128]{1,0:T(8,128)S(1)}, u32[]{:S(2)}, u32[]{:S(2)}) %collective-permute-start.4) | collective-permute-done | bytes 262176 | tf_op jit(solution)/shard_map/ppermute | solution.py:13
  6.8 1.6 pad_maximum_fusion
  9.3 1.3 add_multiply_fusion.2
  10.6 3.6 %collective-permute-start.5 = (f32[512,128]{1,0:T(8,128)S(1)}, f32[512,128]{1,0:T(8,128)S(1)}, u32[]{:S(2)}, u32[]{:S(2)}) collective-permute-start(f32[512,128]{1,0:T(8,128)S(1)} %add_bitcast_fusion), channel_id=1, source_target_pairs={{0,1},{1,2},{2,3},{3,4},{4,5},{5,6},{6,7},{7,8},{8,9},{9,10},{10,1... | collective-permute-start | bytes 786440 | tf_op jit(solution)/shard_map/ppermute | solution.py:13
  14.3 1.5 collective-permute-start
  15.7 1.9 collective-permute-start.1
  18.6 3.3 %collective-permute-start.6 = (f32[3072,128]{1,0:T(8,128)S(1)}, f32[3072,128]{1,0:T(8,128)S(1)}, u32[]{:S(2)}, u32[]{:S(2)}) collective-permute-start(f32[3072,128]{1,0:T(8,128)S(1)} %bitcast.10), channel_id=1, source_target_pairs={{0,64},{64,128},{128,192},{192,0},{1,65},{65,129},{129,193},{193,1... | collective-permute-start | bytes 4718600 | tf_op jit(solution)/shard_map/ppermute | solution.py:75
  22.0 3.1 %collective-permute-start.8 = (f32[3072,128]{1,0:T(8,128)S(1)}, f32[3072,128]{1,0:T(8,128)S(1)}, u32[]{:S(2)}, u32[]{:S(2)}) collective-permute-start(f32[3072,128]{1,0:T(8,128)S(1)} %bitcast.11), channel_id=1, source_target_pairs={{0,192},{64,0},{128,64},{192,128},{1,193},{65,1},{129,65},{193,129... | collective-permute-start | bytes 4718600 | tf_op jit(solution)/shard_map/ppermute | solution.py:76
  25.1 27.1 %collective-permute-done = f32[3072,128]{1,0:T(8,128)S(1)} collective-permute-done((f32[3072,128]{1,0:T(8,128)S(1)}, f32[3072,128]{1,0:T(8,128)S(1)}, u32[]{:S(2)}, u32[]{:S(2)}) %collective-permute-start) | collective-permute-done | bytes 1572896 | tf_op jit(solution)/shard_map/ppermute | solution.py:61
  53.2 1.9 collective-permute-start.2
  55.1 31.6 %collective-permute-done.1 = f32[3072,128]{1,0:T(8,128)S(1)} collective-permute-done((f32[3072,128]{1,0:T(8,128)S(1)}, f32[3072,128]{1,0:T(8,128)S(1)}, u32[]{:S(2)}, u32[]{:S(2)}) %collective-permute-start.1) | collective-permute-done | bytes 1572896 | tf_op jit(solution)/shard_map/ppermute | solution.py:62
  87.7 2.1 collective-permute-start.3
  89.9 52.8 %collective-permute-done.6 = f32[3072,128]{1,0:T(8,128)S(1)} collective-permute-done((f32[3072,128]{1,0:T(8,128)S(1)}, f32[3072,128]{1,0:T(8,128)S(1)}, u32[]{:S(2)}, u32[]{:S(2)}) %collective-permute-start.6) | collective-permute-done | bytes 1572896 | tf_op jit(solution)/shard_map/ppermute | solution.py:75
  144.7 4.1 %collective-permute-start.9 = (f32[1536,128]{1,0:T(8,128)}, f32[1536,128]{1,0:T(8,128)}, u32[]{:S(2)}, u32[]{:S(2)}) collective-permute-start(f32[1536,128]{1,0:T(8,128)} %slice.56), channel_id=1, source_target_pairs={{0,192},{64,0},{128,64},{192,128},{1,193},{65,1},{129,65},{193,129... | collective-permute-start | bytes 2359304 | tf_op jit(solution)/shard_map/ppermute | solution.py:80
  148.8 4.9 %collective-permute-done.2 = f32[1536,128]{1,0:T(8,128)} collective-permute-done((f32[1536,128]{1,0:T(8,128)}, f32[1536,128]{1,0:T(8,128)}, u32[]{:S(2)}, u32[]{:S(2)}) %collective-permute-start.2) | collective-permute-done | bytes 786464 | tf_op jit(solution)/shard_map/ppermute | solution.py:65
  153.7 21.4 %collective-permute-done.7 = f32[1536,128]{1,0:T(8,128)} collective-permute-done((f32[1536,128]{1,0:T(8,128)}, f32[1536,128]{1,0:T(8,128)}, u32[]{:S(2)}, u32[]{:S(2)}) %collective-permute-start.7) | collective-permute-done | bytes 786464 | tf_op jit(solution)/shard_map/ppermute | solution.py:79
  175.2 8.8 %fusion = f32[512,512]{1,0:T(8,128)S(1)} fusion(f32[1536,128]{1,0:T(8,128)} %collective-permute-done.3, f32[1536,128]{1,0:T(8,128)} %collective-permute-done.2, f32[3072,128]{1,0:T(8,128)} %copy-done.3, f32[3072,128]{1,0:T(8,128)} %copy-done.2, f32[3072,128]{1,0:T(8,128)S(1)} %copy-done, f32[3072,128]{1,0:T(8,128)} %copy-done.5, ...), kind=kOutput, calls=%fused_computation | convolution fusion | flops 4844421120 | bytes 13631488 | tf_op jit(solution)/shard_map/dot_general | solution.py:46
  185.0 1.9 collective-permute-start.10
  187.7 1.9 collective-permute-start.13
  189.6 4.9 %collective-permute-start.14 = (f32[128,128]{1,0:T(8,128)S(1)}, f32[128,128]{1,0:T(8,128)S(1)}, u32[]{:S(2)}, u32[]{:S(2)}) collective-permute-start(f32[128,128]{1,0:T(8,128)S(1)} %get-tuple-element.23), channel_id=1, source_target_pairs={{0,16},{1,20},{2,24},{3,28},{4,32},{5,36},{6,40},{7,44},{8,48},{9,... | collective-permute-start | bytes 196616 | tf_op jit(solution)/shard_map/ppermute | solution.py:120
  194.5 5.0 %collective-permute-start.15 = (f32[128,128]{1,0:T(8,128)S(1)}, f32[128,128]{1,0:T(8,128)S(1)}, u32[]{:S(2)}, u32[]{:S(2)}) collective-permute-start(f32[128,128]{1,0:T(8,128)S(1)} %get-tuple-element.22), channel_id=1, source_target_pairs={{0,20},{1,24},{2,28},{3,32},{4,36},{5,40},{6,44},{7,48},{8,52},{9,... | collective-permute-start | bytes 196616 | tf_op jit(solution)/shard_map/ppermute | solution.py:120
  199.5 4.0 %collective-permute-start.16 = (f32[128,128]{1,0:T(8,128)S(1)}, f32[128,128]{1,0:T(8,128)S(1)}, u32[]{:S(2)}, u32[]{:S(2)}) collective-permute-start(f32[128,128]{1,0:T(8,128)S(1)} %get-tuple-element.21), channel_id=1, source_target_pairs={{0,24},{1,28},{2,32},{3,36},{4,40},{5,44},{6,48},{7,52},{8,56},{9,... | collective-permute-start | bytes 196616 | tf_op jit(solution)/shard_map/ppermute | solution.py:120
  204.6 1.9 collective-permute-start.17
  206.6 3.8 %collective-permute-start.11 = (f32[128,128]{1,0:T(8,128)S(1)}, f32[128,128]{1,0:T(8,128)S(1)}, u32[]{:S(2)}, u32[]{:S(2)}) collective-permute-start(f32[128,128]{1,0:T(8,128)S(1)} %get-tuple-element.10), channel_id=1, source_target_pairs={{0,4},{1,8},{2,12},{3,16},{4,20},{5,24},{6,28},{7,32},{8,36},{9,40... | collective-permute-start | bytes 196616 | tf_op jit(solution)/shard_map/ppermute | solution.py:120
  211.5 4.9 %collective-permute-start.19 = (f32[128,128]{1,0:T(8,128)S(1)}, f32[128,128]{1,0:T(8,128)S(1)}, u32[]{:S(2)}, u32[]{:S(2)}) collective-permute-start(f32[128,128]{1,0:T(8,128)S(1)} %get-tuple-element.17), channel_id=1, source_target_pairs={{0,36},{1,40},{2,44},{3,48},{4,52},{5,56},{6,60},{7,0},{8,4},{9,8}... | collective-permute-start | bytes 196616 | tf_op jit(solution)/shard_map/ppermute | solution.py:120
  216.3 4.8 %collective-permute-start.20 = (f32[128,128]{1,0:T(8,128)S(1)}, f32[128,128]{1,0:T(8,128)S(1)}, u32[]{:S(2)}, u32[]{:S(2)}) collective-permute-start(f32[128,128]{1,0:T(8,128)S(1)} %get-tuple-element.16), channel_id=1, source_target_pairs={{0,40},{1,44},{2,48},{3,52},{4,56},{5,60},{6,0},{7,4},{8,8},{9,12}... | collective-permute-start | bytes 196616 | tf_op jit(solution)/shard_map/ppermute | solution.py:120
  221.2 3.7 %collective-permute-start.22 = (f32[128,128]{1,0:T(8,128)S(1)}, f32[128,128]{1,0:T(8,128)S(1)}, u32[]{:S(2)}, u32[]{:S(2)}) collective-permute-start(f32[128,128]{1,0:T(8,128)S(1)} %get-tuple-element.14), channel_id=1, source_target_pairs={{0,48},{1,52},{2,56},{3,60},{4,0},{5,4},{6,8},{7,12},{8,16},{9,20}... | collective-permute-start | bytes 196616 | tf_op jit(solution)/shard_map/ppermute | solution.py:120
  224.9 3.1 %collective-permute-start.23 = (f32[128,128]{1,0:T(8,128)S(1)}, f32[128,128]{1,0:T(8,128)S(1)}, u32[]{:S(2)}, u32[]{:S(2)}) collective-permute-start(f32[128,128]{1,0:T(8,128)S(1)} %get-tuple-element.13), channel_id=1, source_target_pairs={{0,52},{1,56},{2,60},{3,0},{4,4},{5,8},{6,12},{7,16},{8,20},{9,24}... | collective-permute-start | bytes 196616 | tf_op jit(solution)/shard_map/ppermute | solution.py:120
  228.0 6.5 %collective-permute-start.24 = (f32[128,128]{1,0:T(8,128)S(1)}, f32[128,128]{1,0:T(8,128)S(1)}, u32[]{:S(2)}, u32[]{:S(2)}) collective-permute-start(f32[128,128]{1,0:T(8,128)S(1)} %get-tuple-element.12), channel_id=1, source_target_pairs={{0,56},{1,60},{2,0},{3,4},{4,8},{5,12},{6,16},{7,20},{8,24},{9,28}... | collective-permute-start | bytes 196616 | tf_op jit(solution)/shard_map/ppermute | solution.py:120
  234.5 3.6 %collective-permute-done.24 = f32[128,128]{1,0:T(8,128)S(1)} collective-permute-done((f32[128,128]{1,0:T(8,128)S(1)}, f32[128,128]{1,0:T(8,128)S(1)}, u32[]{:S(2)}, u32[]{:S(2)}) %collective-permute-start.24) | collective-permute-done | bytes 65568 | tf_op jit(solution)/shard_map/ppermute | solution.py:120
  238.1 4.6 %collective-permute-done.25 = f32[128,128]{1,0:T(8,128)S(1)} collective-permute-done((f32[128,128]{1,0:T(8,128)S(1)}, f32[128,128]{1,0:T(8,128)S(1)}, u32[]{:S(2)}, u32[]{:S(2)}) %collective-permute-start.25) | collective-permute-done | bytes 65568 | tf_op jit(solution)/shard_map/ppermute | solution.py:120
  (50 shorter events, 11.9 us)
Async XLA Ops:
  1.0 5.8 %collective-permute-start.4 = (f32[512,128]{1,0:T(8,128)S(1)}, f32[512,128]{1,0:T(8,128)S(1)}, u32[]{:S(2)}, u32[]{:S(2)}) collective-permute-start(f32[512,128]{1,0:T(8,128)S(1)} %slice.42), channel_id=1, source_target_pairs={{1,0},{2,1},{3,2},{4,3},{5,4},{6,5},{7,6},{8,7},{9,8},{10,9},{11,1... | collective-permute-start | bytes 786440 | tf_op jit(solution)/shard_map/ppermute | solution.py:13
  6.8 1.9 copy-start
  10.6 7.9 %collective-permute-start.5 = (f32[512,128]{1,0:T(8,128)S(1)}, f32[512,128]{1,0:T(8,128)S(1)}, u32[]{:S(2)}, u32[]{:S(2)}) collective-permute-start(f32[512,128]{1,0:T(8,128)S(1)} %add_bitcast_fusion), channel_id=1, source_target_pairs={{0,1},{1,2},{2,3},{3,4},{4,5},{5,6},{6,7},{7,8},{8,9},{9,10},{10,1... | collective-permute-start | bytes 786440 | tf_op jit(solution)/shard_map/ppermute | solution.py:13
  14.3 37.9 %collective-permute-start = (f32[3072,128]{1,0:T(8,128)S(1)}, f32[3072,128]{1,0:T(8,128)S(1)}, u32[]{:S(2)}, u32[]{:S(2)}) collective-permute-start(f32[3072,128]{1,0:T(8,128)S(1)} %copy-done), channel_id=1, source_target_pairs={{0,16},{16,0},{32,48},{48,32},{1,17},{17,1},{33,49},{49,33},{2,18}... | collective-permute-start | bytes 4718600 | tf_op jit(solution)/shard_map/ppermute | solution.py:61
  15.7 71.0 %collective-permute-start.1 = (f32[3072,128]{1,0:T(8,128)S(1)}, f32[3072,128]{1,0:T(8,128)S(1)}, u32[]{:S(2)}, u32[]{:S(2)}) collective-permute-start(f32[3072,128]{1,0:T(8,128)S(1)} %copy-done), channel_id=1, source_target_pairs={{0,32},{16,48},{32,0},{48,16},{1,33},{17,49},{33,1},{49,17},{2,34}... | collective-permute-start | bytes 4718600 | tf_op jit(solution)/shard_map/ppermute | solution.py:62
  18.6 124.0 %collective-permute-start.6 = (f32[3072,128]{1,0:T(8,128)S(1)}, f32[3072,128]{1,0:T(8,128)S(1)}, u32[]{:S(2)}, u32[]{:S(2)}) collective-permute-start(f32[3072,128]{1,0:T(8,128)S(1)} %bitcast.10), channel_id=1, source_target_pairs={{0,64},{64,128},{128,192},{192,0},{1,65},{65,129},{129,193},{193,1... | collective-permute-start | bytes 4718600 | tf_op jit(solution)/shard_map/ppermute | solution.py:75
  22.0 121.7 %collective-permute-start.8 = (f32[3072,128]{1,0:T(8,128)S(1)}, f32[3072,128]{1,0:T(8,128)S(1)}, u32[]{:S(2)}, u32[]{:S(2)}) collective-permute-start(f32[3072,128]{1,0:T(8,128)S(1)} %bitcast.11), channel_id=1, source_target_pairs={{0,192},{64,0},{128,64},{192,128},{1,193},{65,1},{129,65},{193,129... | collective-permute-start | bytes 4718600 | tf_op jit(solution)/shard_map/ppermute | solution.py:76
  52.2 35.6 %copy-start.2 = (f32[3072,128]{1,0:T(8,128)}, f32[3072,128]{1,0:T(8,128)S(1)}, u32[]{:S(2)}) copy-start(f32[3072,128]{1,0:T(8,128)S(1)} %collective-permute-done) | copy-start | bytes 4718596
  53.2 100.6 %collective-permute-start.2 = (f32[1536,128]{1,0:T(8,128)}, f32[1536,128]{1,0:T(8,128)}, u32[]{:S(2)}, u32[]{:S(2)}) collective-permute-start(f32[1536,128]{1,0:T(8,128)} %slice.51), channel_id=1, source_target_pairs={{0,32},{16,48},{32,0},{48,16},{1,33},{17,49},{33,1},{49,17},{2,34}... | collective-permute-start | bytes 2359304 | tf_op jit(solution)/shard_map/ppermute | solution.py:65
  86.7 56.9 %copy-start.3 = (f32[3072,128]{1,0:T(8,128)}, f32[3072,128]{1,0:T(8,128)S(1)}, u32[]{:S(2)}) copy-start(f32[3072,128]{1,0:T(8,128)S(1)} %collective-permute-done.1) | copy-start | bytes 4718596
  87.7 66.0 %collective-permute-start.3 = (f32[1536,128]{1,0:T(8,128)}, f32[1536,128]{1,0:T(8,128)}, u32[]{:S(2)}, u32[]{:S(2)}) collective-permute-start(f32[1536,128]{1,0:T(8,128)} %slice.52), channel_id=1, source_target_pairs={{0,16},{16,0},{32,48},{48,32},{1,17},{17,1},{33,49},{49,33},{2,18}... | collective-permute-start | bytes 2359304 | tf_op jit(solution)/shard_map/ppermute | solution.py:66
  142.6 2.1 copy-start.4
  143.6 31.5 %collective-permute-start.7 = (f32[1536,128]{1,0:T(8,128)}, f32[1536,128]{1,0:T(8,128)}, u32[]{:S(2)}, u32[]{:S(2)}) collective-permute-start(f32[1536,128]{1,0:T(8,128)} %slice.55), channel_id=1, source_target_pairs={{0,64},{64,128},{128,192},{192,0},{1,65},{65,129},{129,193},{193,1... | collective-permute-start | bytes 2359304 | tf_op jit(solution)/shard_map/ppermute | solution.py:79
  143.6 5.2 %copy-start.5 = (f32[3072,128]{1,0:T(8,128)}, f32[3072,128]{1,0:T(8,128)S(1)}, u32[]{:S(2)}) copy-start(f32[3072,128]{1,0:T(8,128)S(1)} %collective-permute-done.8) | copy-start | bytes 4718596
  144.7 30.5 %collective-permute-start.9 = (f32[1536,128]{1,0:T(8,128)}, f32[1536,128]{1,0:T(8,128)}, u32[]{:S(2)}, u32[]{:S(2)}) collective-permute-start(f32[1536,128]{1,0:T(8,128)} %slice.56), channel_id=1, source_target_pairs={{0,192},{64,0},{128,64},{192,128},{1,193},{65,1},{129,65},{193,129... | collective-permute-start | bytes 2359304 | tf_op jit(solution)/shard_map/ppermute | solution.py:80
  184.0 1.0 copy-start.1
  185.0 14.4 %collective-permute-start.10 = (f32[128,128]{1,0:T(8,128)S(1)}, f32[128,128]{1,0:T(8,128)S(1)}, u32[]{:S(2)}, u32[]{:S(2)}) collective-permute-start(f32[128,128]{1,0:T(8,128)S(1)} %get-tuple-element.19), channel_id=1, source_target_pairs={{0,0},{1,4},{2,8},{3,12},{4,16},{5,20},{6,24},{7,28},{8,32},{9,36}... | collective-permute-start | bytes 196616 | tf_op jit(solution)/shard_map/ppermute | solution.py:120
  187.6 17.0 %collective-permute-start.12 = (f32[128,128]{1,0:T(8,128)S(1)}, f32[128,128]{1,0:T(8,128)S(1)}, u32[]{:S(2)}, u32[]{:S(2)}) collective-permute-start(f32[128,128]{1,0:T(8,128)S(1)} %get-tuple-element.25), channel_id=1, source_target_pairs={{0,8},{1,12},{2,16},{3,20},{4,24},{5,28},{6,32},{7,36},{8,40},{9,4... | collective-permute-start | bytes 196616 | tf_op jit(solution)/shard_map/ppermute | solution.py:120
  187.7 18.9 %collective-permute-start.13 = (f32[128,128]{1,0:T(8,128)S(1)}, f32[128,128]{1,0:T(8,128)S(1)}, u32[]{:S(2)}, u32[]{:S(2)}) collective-permute-start(f32[128,128]{1,0:T(8,128)S(1)} %get-tuple-element.24), channel_id=1, source_target_pairs={{0,12},{1,16},{2,20},{3,24},{4,28},{5,32},{6,36},{7,40},{8,44},{9,... | collective-permute-start | bytes 196616 | tf_op jit(solution)/shard_map/ppermute | solution.py:120
  189.6 20.8 %collective-permute-start.14 = (f32[128,128]{1,0:T(8,128)S(1)}, f32[128,128]{1,0:T(8,128)S(1)}, u32[]{:S(2)}, u32[]{:S(2)}) collective-permute-start(f32[128,128]{1,0:T(8,128)S(1)} %get-tuple-element.23), channel_id=1, source_target_pairs={{0,16},{1,20},{2,24},{3,28},{4,32},{5,36},{6,40},{7,44},{8,48},{9,... | collective-permute-start | bytes 196616 | tf_op jit(solution)/shard_map/ppermute | solution.py:120
  194.5 17.0 %collective-permute-start.15 = (f32[128,128]{1,0:T(8,128)S(1)}, f32[128,128]{1,0:T(8,128)S(1)}, u32[]{:S(2)}, u32[]{:S(2)}) collective-permute-start(f32[128,128]{1,0:T(8,128)S(1)} %get-tuple-element.22), channel_id=1, source_target_pairs={{0,20},{1,24},{2,28},{3,32},{4,36},{5,40},{6,44},{7,48},{8,52},{9,... | collective-permute-start | bytes 196616 | tf_op jit(solution)/shard_map/ppermute | solution.py:120
  199.5 16.8 %collective-permute-start.16 = (f32[128,128]{1,0:T(8,128)S(1)}, f32[128,128]{1,0:T(8,128)S(1)}, u32[]{:S(2)}, u32[]{:S(2)}) collective-permute-start(f32[128,128]{1,0:T(8,128)S(1)} %get-tuple-element.21), channel_id=1, source_target_pairs={{0,24},{1,28},{2,32},{3,36},{4,40},{5,44},{6,48},{7,52},{8,56},{9,... | collective-permute-start | bytes 196616 | tf_op jit(solution)/shard_map/ppermute | solution.py:120
  204.6 16.5 %collective-permute-start.17 = (f32[128,128]{1,0:T(8,128)S(1)}, f32[128,128]{1,0:T(8,128)S(1)}, u32[]{:S(2)}, u32[]{:S(2)}) collective-permute-start(f32[128,128]{1,0:T(8,128)S(1)} %get-tuple-element.20), channel_id=1, source_target_pairs={{0,28},{1,32},{2,36},{3,40},{4,44},{5,48},{6,52},{7,56},{8,60},{9,... | collective-permute-start | bytes 196616 | tf_op jit(solution)/shard_map/ppermute | solution.py:120
  206.6 14.6 %collective-permute-start.11 = (f32[128,128]{1,0:T(8,128)S(1)}, f32[128,128]{1,0:T(8,128)S(1)}, u32[]{:S(2)}, u32[]{:S(2)}) collective-permute-start(f32[128,128]{1,0:T(8,128)S(1)} %get-tuple-element.10), channel_id=1, source_target_pairs={{0,4},{1,8},{2,12},{3,16},{4,20},{5,24},{6,28},{7,32},{8,36},{9,40... | collective-permute-start | bytes 196616 | tf_op jit(solution)/shard_map/ppermute | solution.py:120
  210.4 14.5 %collective-permute-start.18 = (f32[128,128]{1,0:T(8,128)S(1)}, f32[128,128]{1,0:T(8,128)S(1)}, u32[]{:S(2)}, u32[]{:S(2)}) collective-permute-start(f32[128,128]{1,0:T(8,128)S(1)} %get-tuple-element.18), channel_id=1, source_target_pairs={{0,32},{1,36},{2,40},{3,44},{4,48},{5,52},{6,56},{7,60},{8,0},{9,4... | collective-permute-start | bytes 196616 | tf_op jit(solution)/shard_map/ppermute | solution.py:120
  211.5 16.5 %collective-permute-start.19 = (f32[128,128]{1,0:T(8,128)S(1)}, f32[128,128]{1,0:T(8,128)S(1)}, u32[]{:S(2)}, u32[]{:S(2)}) collective-permute-start(f32[128,128]{1,0:T(8,128)S(1)} %get-tuple-element.17), channel_id=1, source_target_pairs={{0,36},{1,40},{2,44},{3,48},{4,52},{5,56},{6,60},{7,0},{8,4},{9,8}... | collective-permute-start | bytes 196616 | tf_op jit(solution)/shard_map/ppermute | solution.py:120
  216.3 18.1 %collective-permute-start.20 = (f32[128,128]{1,0:T(8,128)S(1)}, f32[128,128]{1,0:T(8,128)S(1)}, u32[]{:S(2)}, u32[]{:S(2)}) collective-permute-start(f32[128,128]{1,0:T(8,128)S(1)} %get-tuple-element.16), channel_id=1, source_target_pairs={{0,40},{1,44},{2,48},{3,52},{4,56},{5,60},{6,0},{7,4},{8,8},{9,12}... | collective-permute-start | bytes 196616 | tf_op jit(solution)/shard_map/ppermute | solution.py:120
  221.1 13.4 %collective-permute-start.21 = (f32[128,128]{1,0:T(8,128)S(1)}, f32[128,128]{1,0:T(8,128)S(1)}, u32[]{:S(2)}, u32[]{:S(2)}) collective-permute-start(f32[128,128]{1,0:T(8,128)S(1)} %get-tuple-element.15), channel_id=1, source_target_pairs={{0,44},{1,48},{2,52},{3,56},{4,60},{5,0},{6,4},{7,8},{8,12},{9,16}... | collective-permute-start | bytes 196616 | tf_op jit(solution)/shard_map/ppermute | solution.py:120
  221.2 13.3 %collective-permute-start.22 = (f32[128,128]{1,0:T(8,128)S(1)}, f32[128,128]{1,0:T(8,128)S(1)}, u32[]{:S(2)}, u32[]{:S(2)}) collective-permute-start(f32[128,128]{1,0:T(8,128)S(1)} %get-tuple-element.14), channel_id=1, source_target_pairs={{0,48},{1,52},{2,56},{3,60},{4,0},{5,4},{6,8},{7,12},{8,16},{9,20}... | collective-permute-start | bytes 196616 | tf_op jit(solution)/shard_map/ppermute | solution.py:120
  224.9 9.6 %collective-permute-start.23 = (f32[128,128]{1,0:T(8,128)S(1)}, f32[128,128]{1,0:T(8,128)S(1)}, u32[]{:S(2)}, u32[]{:S(2)}) collective-permute-start(f32[128,128]{1,0:T(8,128)S(1)} %get-tuple-element.13), channel_id=1, source_target_pairs={{0,52},{1,56},{2,60},{3,0},{4,4},{5,8},{6,12},{7,16},{8,20},{9,24}... | collective-permute-start | bytes 196616 | tf_op jit(solution)/shard_map/ppermute | solution.py:120
  228.0 10.1 %collective-permute-start.24 = (f32[128,128]{1,0:T(8,128)S(1)}, f32[128,128]{1,0:T(8,128)S(1)}, u32[]{:S(2)}, u32[]{:S(2)}) collective-permute-start(f32[128,128]{1,0:T(8,128)S(1)} %get-tuple-element.12), channel_id=1, source_target_pairs={{0,56},{1,60},{2,0},{3,4},{4,8},{5,12},{6,16},{7,20},{8,24},{9,28}... | collective-permute-start | bytes 196616 | tf_op jit(solution)/shard_map/ppermute | solution.py:120
  234.5 8.2 %collective-permute-start.25 = (f32[128,128]{1,0:T(8,128)S(1)}, f32[128,128]{1,0:T(8,128)S(1)}, u32[]{:S(2)}, u32[]{:S(2)}) collective-permute-start(f32[128,128]{1,0:T(8,128)S(1)} %get-tuple-element.11), channel_id=1, source_target_pairs={{0,60},{1,0},{2,4},{3,8},{4,12},{5,16},{6,20},{7,24},{8,28},{9,32}... | collective-permute-start | bytes 196616 | tf_op jit(solution)/shard_map/ppermute | solution.py:120

commit v5 on v4

--- a/solution.py
+++ b/solution.py
@@ -1,8 +1,11 @@
+import functools
 import math
 
 import jax
 import jax.numpy as jnp
 from jax import lax
+from jax.experimental import pallas as pl
+from jax.experimental.pallas import tpu as pltpu
 from jax.sharding import Mesh
 from jax.sharding import PartitionSpec as P
 
@@ -84,6 +87,89 @@
     return jnp.concatenate([block, from_left, far, from_right], 1)
 
 
+def two_bit_xor(a, b):
+    both = (a % 2) * (b % 2) + 2 * ((a // 2) * (b // 2))
+    return a + b - 2 * both
+
+
+def owners_kernel(side, tiles, part_ref, out_ref, slots, send_sems, recv_sems):
+    me_r, me_c, me_t = lax.axis_index("r"), lax.axis_index("c"), lax.axis_index("mesh")
+    width = out_ref.shape[0]
+    mine = (me_t % side) == me_c
+    sends = []
+    for j in range(tiles):
+        row_block = two_bit_xor(me_c, j // side)
+        col_block = (me_r - j % side + side) % side
+        dest_t = me_c + side * (j % side)
+        to_self = jnp.logical_and(me_c == j // side, dest_t == me_t)
+        copy = pltpu.make_async_remote_copy(
+            src_ref=part_ref.at[
+                pl.ds(pl.multiple_of(row_block * width, width), width),
+                pl.ds(pl.multiple_of(col_block * width, width), width),
+            ],
+            dst_ref=slots.at[me_t],
+            send_sem=send_sems.at[j],
+            recv_sem=recv_sems.at[me_t],
+            device_id=(me_r, j // side, dest_t),
+            device_id_type=pl.DeviceIdType.MESH,
+        )
+        sends.append((copy, to_self, row_block, col_block))
+
+        @pl.when(jnp.logical_not(to_self))
+        def _():
+            copy.start()
+
+    for j, (copy, to_self, row_block, col_block) in enumerate(sends):
+
+        @pl.when(to_self)
+        def _():
+            slots[me_t] = part_ref[
+                pl.ds(pl.multiple_of(row_block * width, width), width),
+                pl.ds(pl.multiple_of(col_block * width, width), width),
+            ]
+
+    for source in range(tiles):
+        arrival = pltpu.make_async_remote_copy(
+            src_ref=slots.at[source],
+            dst_ref=slots.at[source],
+            send_sem=send_sems.at[source],
+            recv_sem=recv_sems.at[source],
+            device_id=(me_r, me_c, me_t),
+            device_id_type=pl.DeviceIdType.MESH,
+        )
+
+        @pl.when(jnp.logical_not(jnp.logical_and(mine, me_t == source)))
+        def _():
+            arrival.wait_recv()
+
+    for copy, to_self, _, _ in sends:
+
+        @pl.when(jnp.logical_not(to_self))
+        def _():
+            copy.wait_send()
+
+    acc = slots[0]
+    for source in range(1, tiles):
+        acc = acc + slots[source]
+    out_ref[...] = acc
+
+
+def scatter_to_owners(partial_value, side, tiles):
+    width = partial_value.shape[0] // side
+    return pl.pallas_call(
+        functools.partial(owners_kernel, side, tiles),
+        out_shape=jax.ShapeDtypeStruct((width, width), jnp.float32),
+        in_specs=[pl.BlockSpec(memory_space=pltpu.VMEM)],
+        out_specs=pl.BlockSpec(memory_space=pltpu.VMEM),
+        scratch_shapes=[
+            pltpu.VMEM((tiles, width, width), jnp.float32),
+            pltpu.SemaphoreType.DMA((tiles,)),
+            pltpu.SemaphoreType.DMA((tiles,)),
+        ],
+        compiler_params=pltpu.CompilerParams(has_side_effects=True),
+    )(partial_value)
+
+
 def local(snapshots, region_ids, conductivity):
     strip, width = region_ids.shape
     node_rows, group_cols = snapshots.shape
@@ -101,24 +187,7 @@
     rows = square_gather(snapshots, "c")
     cols = ring_gather(panel, "r")
     partial_value = contract(rows, cols)
-    me_r, me_c, me_t = lax.axis_index("r"), lax.axis_index("c"), lax.axis_index("mesh")
-
-    def piece_of(j):
-        row_block = jnp.bitwise_xor(me_c, j // side)
-        col_block = (me_r - j % side) % side
-        return lax.dynamic_slice(
-            partial_value, (row_block * group_cols, col_block * group_cols), (group_cols, group_cols)
-        )
-
-    placed = None
-    for step in range(tiles):
-        perm = []
-        for c in range(side):
-            for t in range(tiles):
-                j = (t + step) % tiles
-                perm.append((c * tiles + t, (j // side) * tiles + c + side * (j % side)))
-        moved = lax.ppermute(piece_of((me_t + step) % tiles), ("c", "mesh"), perm)
-        placed = moved if placed is None else placed + moved
+    placed = scatter_to_owners(partial_value, side, tiles)
     total_nodes = node_rows * tiles
     return placed / math.sqrt(total_nodes)
 

time: 244 us -> 219 us (0.90)
  the two profiles are of different devices: /device:TPU:22 before, /device:TPU:31 now
where the time goes in v5:
time: 219 us
  waiting for transfers between devices  140 us (64%)
  Pallas kernels  44.3 us (20%)
  starting transfers between devices  20.5 us (9%)
  other arithmetic  6.66 us (3%)
  matrix products  6.31 us (3%)
    ppermute x1, waiting for transfers between devices, ring_gather(): lax.ppermute(block, axis, pairs(count, lambda i: (i + 1) % count))  45.4 us
    pallas_call x1, Pallas kernels, scatter_to_owners(): pl.pallas_call(functools.partial(owners_kernel, side, tiles), out_shape=j...  44.3 us
    ppermute x1, waiting for transfers between devices, square_gather(): from_z = lax.ppermute(block, axis, pairs(count, lambda i: i ^ 2))  31.6 us
    ppermute x1, waiting for transfers between devices, square_gather(): from_x = lax.ppermute(block, axis, pairs(count, lambda i: i ^ 1))  23 us
    ppermute x1, waiting for transfers between devices, ring_gather(): lax.ppermute(from_left[:half], axis, pairs(count, lambda i: (i + 1) % cou...  22.7 us
    ppermute x1, waiting for transfers between devices, square_gather(): lax.ppermute(from_x[:half], axis, pairs(count, lambda i: i ^ 2))  15.1 us
    dot_general x1, matrix products, contract(): lax.dot_general(left, right, (((0,), (0,)), ((), ())), precision=lax.Prec...  6.31 us
  transfers between devices with their start and end apart: 10, of which 7 were waited for; matrix products, arithmetic and copies ran while one was open for 1% of the time, Pallas kernels for 0%

profile of v5, /device:TPU:31, one launch (start us, length us, event | category | flops | bytes accessed | tf_op | source)
XLA Modules:
  0.0 218.8 jit_solution(6679937335246069861)
XLA Ops:
  0.0 1.0 slice.42
  1.0 2.6 %collective-permute-start.4 = (f32[512,128]{1,0:T(8,128)S(1)}, f32[512,128]{1,0:T(8,128)S(1)}, u32[]{:S(2)}, u32[]{:S(2)}) collective-permute-start(f32[512,128]{1,0:T(8,128)S(1)} %slice.42), channel_id=1, source_target_pairs={{1,0},{2,1},{3,2},{4,3},{5,4},{6,5},{7,6},{8,7},{9,8},{10,9},{11,1... | collective-permute-start | bytes 786440 | tf_op jit(solution)/shard_map/ppermute | solution.py:16
  3.6 0.8 select_reduce_fusion
  4.4 0.3 collective-permute-done.4
  4.7 1.6 pad_maximum_fusion
  6.4 0.2 copy-done
  6.6 0.8 add_multiply_fusion.3
  7.4 1.4 add_multiply_fusion.2
  8.8 1.3 collective-permute-start.5
  10.1 1.2 collective-permute-start
  11.4 1.6 collective-permute-start.1
  13.0 0.3 pad_add_fusion
  13.3 1.4 collective-permute-done.5
  14.7 0.1 add_add_fusion
  14.7 0.1 pad_maximum_fusion.1
  14.9 3.1 %collective-permute-start.6 = (f32[3072,128]{1,0:T(8,128)S(1)}, f32[3072,128]{1,0:T(8,128)S(1)}, u32[]{:S(2)}, u32[]{:S(2)}) collective-permute-start(f32[3072,128]{1,0:T(8,128)S(1)} %bitcast.10), channel_id=1, source_target_pairs={{0,64},{64,128},{128,192},{192,0},{1,65},{65,129},{129,193},{193,1... | collective-permute-start | bytes 4718600 | tf_op jit(solution)/shard_map/ppermute | solution.py:78
  17.9 3.1 %collective-permute-start.8 = (f32[3072,128]{1,0:T(8,128)S(1)}, f32[3072,128]{1,0:T(8,128)S(1)}, u32[]{:S(2)}, u32[]{:S(2)}) collective-permute-start(f32[3072,128]{1,0:T(8,128)S(1)} %bitcast.11), channel_id=1, source_target_pairs={{0,192},{64,0},{128,64},{192,128},{1,193},{65,1},{129,65},{193,129... | collective-permute-start | bytes 4718600 | tf_op jit(solution)/shard_map/ppermute | solution.py:79
  21.0 23.0 %collective-permute-done = f32[3072,128]{1,0:T(8,128)S(1)} collective-permute-done((f32[3072,128]{1,0:T(8,128)S(1)}, f32[3072,128]{1,0:T(8,128)S(1)}, u32[]{:S(2)}, u32[]{:S(2)}) %collective-permute-start) | collective-permute-done | bytes 1572896 | tf_op jit(solution)/shard_map/ppermute | solution.py:64
  44.1 0.1 slice.51
  44.1 1.7 collective-permute-start.2
  45.9 31.6 %collective-permute-done.1 = f32[3072,128]{1,0:T(8,128)S(1)} collective-permute-done((f32[3072,128]{1,0:T(8,128)S(1)}, f32[3072,128]{1,0:T(8,128)S(1)}, u32[]{:S(2)}, u32[]{:S(2)}) %collective-permute-start.1) | collective-permute-done | bytes 1572896 | tf_op jit(solution)/shard_map/ppermute | solution.py:65
  77.5 0.1 slice.52
  77.5 1.9 collective-permute-start.3
  79.5 45.4 %collective-permute-done.6 = f32[3072,128]{1,0:T(8,128)S(1)} collective-permute-done((f32[3072,128]{1,0:T(8,128)S(1)}, f32[3072,128]{1,0:T(8,128)S(1)}, u32[]{:S(2)}, u32[]{:S(2)}) %collective-permute-start.6) | collective-permute-done | bytes 1572896 | tf_op jit(solution)/shard_map/ppermute | solution.py:78
  124.9 0.1 collective-permute-start.7
  125.0 0.1 slice.56
  125.1 3.8 %collective-permute-start.9 = (f32[1536,128]{1,0:T(8,128)S(1)}, f32[1536,128]{1,0:T(8,128)S(1)}, u32[]{:S(2)}, u32[]{:S(2)}) collective-permute-start(f32[1536,128]{1,0:T(8,128)S(1)} %slice.56), channel_id=1, source_target_pairs={{0,192},{64,0},{128,64},{192,128},{1,193},{65,1},{129,65},{193,129... | collective-permute-start | bytes 2359304 | tf_op jit(solution)/shard_map/ppermute | solution.py:83
  128.9 15.1 %collective-permute-done.2 = f32[1536,128]{1,0:T(8,128)S(1)} collective-permute-done((f32[1536,128]{1,0:T(8,128)S(1)}, f32[1536,128]{1,0:T(8,128)S(1)}, u32[]{:S(2)}, u32[]{:S(2)}) %collective-permute-start.2) | collective-permute-done | bytes 786464 | tf_op jit(solution)/shard_map/ppermute | solution.py:68
  144.0 22.7 %collective-permute-done.7 = f32[1536,128]{1,0:T(8,128)S(1)} collective-permute-done((f32[1536,128]{1,0:T(8,128)S(1)}, f32[1536,128]{1,0:T(8,128)S(1)}, u32[]{:S(2)}, u32[]{:S(2)}) %collective-permute-start.7) | collective-permute-done | bytes 786464 | tf_op jit(solution)/shard_map/ppermute | solution.py:82
  166.7 6.3 %fusion.part_ref = f32[512,512]{1,0:T(8,128)} fusion(f32[1536,128]{1,0:T(8,128)S(1)} %collective-permute-done.3, f32[1536,128]{1,0:T(8,128)S(1)} %collective-permute-done.2, f32[3072,128]{1,0:T(8,128)S(1)} %collective-permute-done.1, f32[3072,128]{1,0:T(8,128)S(1)} %collective-permute-done, f32[3072,128]{1,0:T(8,128)S(1)} %copy-done, ...), kind=kOutput, calls=%fused_computation | convolution fusion | flops 4844421120 | bytes 13631488 | tf_op jit(solution)/shard_map/dot_general | solution.py:49
  173.0 44.3 %shard_map.37 = f32[128,128]{1,0:T(8,128)} custom-call(f32[512,512]{1,0:T(8,128)} %fusion.part_ref), custom_call_target="tpu_custom_call" | custom-call | tf_op jit(solution)/shard_map/pallas_call | solution.py:159
  217.3 1.5 broadcast_multiply_fusion
  (7 shorter events, 0.1 us)
Async XLA Ops:
  1.0 3.7 %collective-permute-start.4 = (f32[512,128]{1,0:T(8,128)S(1)}, f32[512,128]{1,0:T(8,128)S(1)}, u32[]{:S(2)}, u32[]{:S(2)}) collective-permute-start(f32[512,128]{1,0:T(8,128)S(1)} %slice.42), channel_id=1, source_target_pairs={{1,0},{2,1},{3,2},{4,3},{5,4},{6,5},{7,6},{8,7},{9,8},{10,9},{11,1... | collective-permute-start | bytes 786440 | tf_op jit(solution)/shard_map/ppermute | solution.py:16
  4.7 1.9 copy-start
  8.8 5.8 %collective-permute-start.5 = (f32[512,128]{1,0:T(8,128)S(1)}, f32[512,128]{1,0:T(8,128)S(1)}, u32[]{:S(2)}, u32[]{:S(2)}) collective-permute-start(f32[512,128]{1,0:T(8,128)S(1)} %add_bitcast_fusion), channel_id=1, source_target_pairs={{0,1},{1,2},{2,3},{3,4},{4,5},{5,6},{6,7},{7,8},{8,9},{9,10},{10,1... | collective-permute-start | bytes 786440 | tf_op jit(solution)/shard_map/ppermute | solution.py:16
  10.1 33.9 %collective-permute-start = (f32[3072,128]{1,0:T(8,128)S(1)}, f32[3072,128]{1,0:T(8,128)S(1)}, u32[]{:S(2)}, u32[]{:S(2)}) collective-permute-start(f32[3072,128]{1,0:T(8,128)S(1)} %copy-done), channel_id=1, source_target_pairs={{0,16},{16,0},{32,48},{48,32},{1,17},{17,1},{33,49},{49,33},{2,18}... | collective-permute-start | bytes 4718600 | tf_op jit(solution)/shard_map/ppermute | solution.py:64
  11.4 66.1 %collective-permute-start.1 = (f32[3072,128]{1,0:T(8,128)S(1)}, f32[3072,128]{1,0:T(8,128)S(1)}, u32[]{:S(2)}, u32[]{:S(2)}) collective-permute-start(f32[3072,128]{1,0:T(8,128)S(1)} %copy-done), channel_id=1, source_target_pairs={{0,32},{16,48},{32,0},{48,16},{1,33},{17,49},{33,1},{49,17},{2,34}... | collective-permute-start | bytes 4718600 | tf_op jit(solution)/shard_map/ppermute | solution.py:65
  14.9 110.0 %collective-permute-start.6 = (f32[3072,128]{1,0:T(8,128)S(1)}, f32[3072,128]{1,0:T(8,128)S(1)}, u32[]{:S(2)}, u32[]{:S(2)}) collective-permute-start(f32[3072,128]{1,0:T(8,128)S(1)} %bitcast.10), channel_id=1, source_target_pairs={{0,64},{64,128},{128,192},{192,0},{1,65},{65,129},{129,193},{193,1... | collective-permute-start | bytes 4718600 | tf_op jit(solution)/shard_map/ppermute | solution.py:78
  17.9 107.1 %collective-permute-start.8 = (f32[3072,128]{1,0:T(8,128)S(1)}, f32[3072,128]{1,0:T(8,128)S(1)}, u32[]{:S(2)}, u32[]{:S(2)}) collective-permute-start(f32[3072,128]{1,0:T(8,128)S(1)} %bitcast.11), channel_id=1, source_target_pairs={{0,192},{64,0},{128,64},{192,128},{1,193},{65,1},{129,65},{193,129... | collective-permute-start | bytes 4718600 | tf_op jit(solution)/shard_map/ppermute | solution.py:79
  44.1 99.9 %collective-permute-start.2 = (f32[1536,128]{1,0:T(8,128)S(1)}, f32[1536,128]{1,0:T(8,128)S(1)}, u32[]{:S(2)}, u32[]{:S(2)}) collective-permute-start(f32[1536,128]{1,0:T(8,128)S(1)} %slice.51), channel_id=1, source_target_pairs={{0,32},{16,48},{32,0},{48,16},{1,33},{17,49},{33,1},{49,17},{2,34}... | collective-permute-start | bytes 2359304 | tf_op jit(solution)/shard_map/ppermute | solution.py:68
  77.5 66.5 %collective-permute-start.3 = (f32[1536,128]{1,0:T(8,128)S(1)}, f32[1536,128]{1,0:T(8,128)S(1)}, u32[]{:S(2)}, u32[]{:S(2)}) collective-permute-start(f32[1536,128]{1,0:T(8,128)S(1)} %slice.52), channel_id=1, source_target_pairs={{0,16},{16,0},{32,48},{48,32},{1,17},{17,1},{33,49},{49,33},{2,18}... | collective-permute-start | bytes 2359304 | tf_op jit(solution)/shard_map/ppermute | solution.py:69
  124.9 41.8 %collective-permute-start.7 = (f32[1536,128]{1,0:T(8,128)S(1)}, f32[1536,128]{1,0:T(8,128)S(1)}, u32[]{:S(2)}, u32[]{:S(2)}) collective-permute-start(f32[1536,128]{1,0:T(8,128)S(1)} %slice.55), channel_id=1, source_target_pairs={{0,64},{64,128},{128,192},{192,0},{1,65},{65,129},{129,193},{193,1... | collective-permute-start | bytes 2359304 | tf_op jit(solution)/shard_map/ppermute | solution.py:82
  125.1 41.6 %collective-permute-start.9 = (f32[1536,128]{1,0:T(8,128)S(1)}, f32[1536,128]{1,0:T(8,128)S(1)}, u32[]{:S(2)}, u32[]{:S(2)}) collective-permute-start(f32[1536,128]{1,0:T(8,128)S(1)} %slice.56), channel_id=1, source_target_pairs={{0,192},{64,0},{128,64},{192,128},{1,193},{65,1},{129,65},{193,129... | collective-permute-start | bytes 2359304 | tf_op jit(solution)/shard_map/ppermute | solution.py:83

commit v6 on v5

--- a/solution.py
+++ b/solution.py
@@ -170,6 +170,72 @@
     )(partial_value)
 
 
+def gather_kernel(a_ref, b_ref, rows_ref, cols_ref, send_sems, recv_sems):
+    me_r, me_c, me_t = lax.axis_index("r"), lax.axis_index("c"), lax.axis_index("mesh")
+    count = lax.axis_size("r")
+    half = a_ref.shape[0] // 2
+    low, high = pl.ds(0, half), pl.ds(half, half)
+    x_mate = (me_r, me_c + 1 - 2 * (me_c % 2), me_t)
+    z_mate = (me_r, (me_c + 2) % 4, me_t)
+    right = ((me_r + 1) % count, me_c, me_t)
+    left = ((me_r + count - 1) % count, me_c, me_t)
+    rows_ref[0] = a_ref[...]
+    cols_ref[0] = b_ref[...]
+
+    def copy(index, src, dst, device):
+        return pltpu.make_async_remote_copy(
+            src_ref=src,
+            dst_ref=dst,
+            send_sem=send_sems.at[index],
+            recv_sem=recv_sems.at[index],
+            device_id=device,
+            device_id_type=pl.DeviceIdType.MESH,
+        )
+
+    first = [
+        copy(0, a_ref.at[low], rows_ref.at[1, low], x_mate),
+        copy(1, a_ref.at[high], rows_ref.at[2, high], z_mate),
+        copy(2, b_ref.at[low], cols_ref.at[1, low], right),
+        copy(3, b_ref.at[high], cols_ref.at[3, high], left),
+    ]
+    second = [
+        copy(4, a_ref.at[high], rows_ref.at[1, high], x_mate),
+        copy(5, a_ref.at[low], rows_ref.at[2, low], z_mate),
+        copy(6, b_ref.at[high], cols_ref.at[1, high], right),
+        copy(7, b_ref.at[low], cols_ref.at[3, low], left),
+    ]
+    for one in first + second:
+        one.start()
+    relays = [
+        copy(8, rows_ref.at[1, low], rows_ref.at[3, low], z_mate),
+        copy(9, rows_ref.at[2, high], rows_ref.at[3, high], x_mate),
+        copy(10, cols_ref.at[1, low], cols_ref.at[2, low], right),
+        copy(11, cols_ref.at[3, high], cols_ref.at[2, high], left),
+    ]
+    for arrived, relay in zip(first, relays):
+        arrived.wait_recv()
+        relay.start()
+    for one in second + relays:
+        one.wait_recv()
+    for one in first + second + relays:
+        one.wait_send()
+
+
+def gather_both(snapshots, panel):
+    node_rows, group_cols = snapshots.shape
+    stack = jax.ShapeDtypeStruct((4, node_rows, group_cols), jnp.float32)
+    return pl.pallas_call(
+        gather_kernel,
+        out_shape=(stack, stack),
+        in_specs=[pl.BlockSpec(memory_space=pltpu.VMEM)] * 2,
+        out_specs=(pl.BlockSpec(memory_space=pltpu.VMEM),) * 2,
+        scratch_shapes=[pltpu.SemaphoreType.DMA((12,)), pltpu.SemaphoreType.DMA((12,))],
+        compiler_params=pltpu.CompilerParams(
+            has_side_effects=True, vmem_limit_bytes=48 * 1024 * 1024
+        ),
+    )(snapshots, panel)
+
+
 def local(snapshots, region_ids, conductivity):
     strip, width = region_ids.shape
     node_rows, group_cols = snapshots.shape
@@ -184,9 +250,14 @@
     panel = jnp.concatenate([inner[:1] + carried[None], inner[1:]], 0).reshape(
         node_rows, group_cols
     )
-    rows = square_gather(snapshots, "c")
-    cols = ring_gather(panel, "r")
-    partial_value = contract(rows, cols)
+    rows, cols = gather_both(snapshots, panel)
+    partial_value = lax.dot_general(
+        rows,
+        cols,
+        (((1,), (1,)), ((), ())),
+        precision=lax.Precision.HIGH,
+        preferred_element_type=jnp.float32,
+    ).reshape(side * group_cols, side * group_cols)
     placed = scatter_to_owners(partial_value, side, tiles)
     total_nodes = node_rows * tiles
     return placed / math.sqrt(total_nodes)

time: 219 us -> 244 us (1.11)
  Pallas kernels: 44.3 us -> 216 us
  waiting for transfers between devices: 140 us -> 4.51 us
  starting transfers between devices: 20.5 us -> 3.89 us
  matrix products: 6.31 us -> 9.17 us
    pallas_call x0 -> x1, Pallas kernels: none -> 181 us  [gather_both(): pl.pallas_call(gather_kernel, out_shape=(stack, stack), in_specs=[pl.Bloc...]
    ppermute x8 -> x0, waiting for transfers between devices: 138 us -> none  [the longest x1 45.4 us: ring_gather(): lax.ppermute(block, axis, pairs(count, lambda i: (i + 1) % count))]
    ppermute x8 -> x0, starting transfers between devices: 16.6 us -> none  [the longest x1 3.81 us: ring_gather(): lax.ppermute(from_right[half:], axis, pairs(count, lambda i: (i - 1) % co...]
    pallas_call x1, Pallas kernels: 44.3 us -> 35.1 us  [scatter_to_owners(): pl.pallas_call(functools.partial(owners_kernel, side, tiles), out_shape=j...]
    dot_general x1, matrix products: 6.31 us -> 9.17 us  [local(): lax.dot_general(rows, cols, (((1,), (1,)), ((), ())), precision=lax.Preci...]
    ppermute x2, waiting for transfers between devices: 1.67 us -> 4.51 us  [passed_along(): lax.ppermute(value, axis, [(source, source + steps) for source in range(f...]
  transfers between devices with their start and end apart: 10 -> 2, of which waited for: 7 -> 2; matrix products, arithmetic and copies ran while one was open for 1% -> 0% of each run, Pallas kernels for 0% -> 0%
where the time goes in v6:
time: 244 us; the launch traced here: 243 us
  Pallas kernels  216 us (89%)
  matrix products  9.17 us (4%)
  other arithmetic  6.35 us (3%)
  waiting for transfers between devices  4.51 us (2%)
  starting transfers between devices  3.89 us (2%)
  local copies, waits for them, and re-layouts  2.91 us (1%)
    pallas_call x1, Pallas kernels, gather_both(): pl.pallas_call(gather_kernel, out_shape=(stack, stack), in_specs=[pl.Bloc...  181 us
    pallas_call x1, Pallas kernels, scatter_to_owners(): pl.pallas_call(functools.partial(owners_kernel, side, tiles), out_shape=j...  35.1 us
    dot_general x1, matrix products, local(): lax.dot_general(rows, cols, (((1,), (1,)), ((), ())), precision=lax.Preci...  9.17 us
  transfers between devices with their start and end apart: 2, of which 2 were waited for; matrix products, arithmetic and copies ran while one was open for 0% of the time, Pallas kernels for 0%

profile of v6, /device:TPU:31, one launch (start us, length us, event | category | flops | bytes accessed | tf_op | source)
XLA Modules:
  0.0 243.3 jit_solution(7605400529152310750)
XLA Ops:
  0.0 1.0 slice.28
  1.0 2.6 %collective-permute-start = (f32[512,128]{1,0:T(8,128)S(1)}, f32[512,128]{1,0:T(8,128)S(1)}, u32[]{:S(2)}, u32[]{:S(2)}) collective-permute-start(f32[512,128]{1,0:T(8,128)S(1)} %slice.28), channel_id=1, source_target_pairs={{1,0},{2,1},{3,2},{4,3},{5,4},{6,5},{7,6},{8,7},{9,8},{10,9},{11,1... | collective-permute-start | bytes 786440 | tf_op jit(solution)/shard_map/ppermute | solution.py:16
  3.6 0.8 select_reduce_fusion
  4.4 0.3 collective-permute-done
  4.7 0.0 copy-start
  4.7 1.6 pad_maximum_fusion
  6.4 0.2 copy-done
  6.6 0.6 add_multiply_fusion.3
  7.2 1.3 add_multiply_fusion.2
  8.5 1.3 collective-permute-start.1
  9.8 0.3 pad_add_fusion
  10.1 4.2 %collective-permute-done.1 = f32[512,128]{1,0:T(8,128)S(1)} collective-permute-done((f32[512,128]{1,0:T(8,128)S(1)}, f32[512,128]{1,0:T(8,128)S(1)}, u32[]{:S(2)}, u32[]{:S(2)}) %collective-permute-start.1) | collective-permute-done | bytes 262176 | tf_op jit(solution)/shard_map/ppermute | solution.py:16
  14.4 0.1 add_add_fusion
  14.4 0.1 pad_maximum_fusion.1
  14.5 181.3 %shard_map.37 = (f32[4,3072,128]{2,1,0:T(8,128)}, f32[4,3072,128]{2,1,0:T(8,128)}) custom-call(f32[3072,128]{1,0:T(8,128)S(1)} %copy-done, f32[3072,128]{1,0:T(8,128)S(1)} %bitcast.23), custom_call_target="tpu_custom_call" | custom-call | tf_op jit(solution)/shard_map/pallas_call | solution.py:227
  195.9 9.2 %fusion = f32[4,128,4,128]{3,1,2,0:T(8,128)S(1)} fusion(f32[4,3072,128]{2,1,0:T(8,128)} %get-tuple-element.7, f32[4,3072,128]{2,1,0:T(8,128)} %get-tuple-element.8), kind=kOutput, calls=%fused_computation | convolution fusion | flops 4831838208 | bytes 13631488 | tf_op jit(solution)/shard_map/dot_general | solution.py:254
  205.1 0.7 copy.7
  205.7 1.0 copy.13
  206.8 35.1 %shard_map.38 = f32[128,128]{1,0:T(8,128)} custom-call(f32[512,512]{1,0:T(8,128)} %bitcast.25), custom_call_target="tpu_custom_call" | custom-call | tf_op jit(solution)/shard_map/pallas_call | solution.py:159
  241.9 1.5 broadcast_multiply_fusion
  (2 shorter events, 0.0 us)
Async XLA Ops:
  1.0 3.7 %collective-permute-start = (f32[512,128]{1,0:T(8,128)S(1)}, f32[512,128]{1,0:T(8,128)S(1)}, u32[]{:S(2)}, u32[]{:S(2)}) collective-permute-start(f32[512,128]{1,0:T(8,128)S(1)} %slice.28), channel_id=1, source_target_pairs={{1,0},{2,1},{3,2},{4,3},{5,4},{6,5},{7,6},{8,7},{9,8},{10,9},{11,1... | collective-permute-start | bytes 786440 | tf_op jit(solution)/shard_map/ppermute | solution.py:16
  4.7 1.9 copy-start
  8.5 5.8 %collective-permute-start.1 = (f32[512,128]{1,0:T(8,128)S(1)}, f32[512,128]{1,0:T(8,128)S(1)}, u32[]{:S(2)}, u32[]{:S(2)}) collective-permute-start(f32[512,128]{1,0:T(8,128)S(1)} %add_bitcast_fusion), channel_id=1, source_target_pairs={{0,1},{1,2},{2,3},{3,4},{4,5},{5,6},{6,7},{7,8},{8,9},{9,10},{10,1... | collective-permute-start | bytes 786440 | tf_op jit(solution)/shard_map/ppermute | solution.py:16

commit v7 on v5

--- a/solution.py
+++ b/solution.py
@@ -61,30 +61,33 @@
 
 def square_gather(block, axis):
     count, half = lax.axis_size(axis), block.shape[0] // 2
-    from_x = lax.ppermute(block, axis, pairs(count, lambda i: i ^ 1))
-    from_z = lax.ppermute(block, axis, pairs(count, lambda i: i ^ 2))
-    corner = jnp.concatenate(
-        [
-            lax.ppermute(from_x[:half], axis, pairs(count, lambda i: i ^ 2)),
-            lax.ppermute(from_z[half:], axis, pairs(count, lambda i: i ^ 1)),
-        ],
-        0,
-    )
-    return jnp.concatenate([block, from_x, from_z, corner], 1)
+    to_x, to_z = pairs(count, lambda i: i ^ 1), pairs(count, lambda i: i ^ 2)
+    x_low = lax.ppermute(block[:half], axis, to_x)
+    z_high = lax.ppermute(block[half:], axis, to_z)
+    x_high = lax.ppermute(block[half:], axis, to_x)
+    z_low = lax.ppermute(block[:half], axis, to_z)
+    corner = [lax.ppermute(x_low, axis, to_z), lax.ppermute(z_high, axis, to_x)]
+    return [block, [x_low, x_high], [z_low, z_high], corner]
 
 
 def ring_gather(block, axis):
     count, half = lax.axis_size(axis), block.shape[0] // 2
-    from_left = lax.ppermute(block, axis, pairs(count, lambda i: (i + 1) % count))
-    from_right = lax.ppermute(block, axis, pairs(count, lambda i: (i - 1) % count))
-    far = jnp.concatenate(
-        [
-            lax.ppermute(from_left[:half], axis, pairs(count, lambda i: (i + 1) % count)),
-            lax.ppermute(from_right[half:], axis, pairs(count, lambda i: (i - 1) % count)),
-        ],
-        0,
-    )
-    return jnp.concatenate([block, from_left, far, from_right], 1)
+    up = pairs(count, lambda i: (i + 1) % count)
+    down = pairs(count, lambda i: (i - 1) % count)
+    left_low = lax.ppermute(block[:half], axis, up)
+    right_high = lax.ppermute(block[half:], axis, down)
+    left_high = lax.ppermute(block[half:], axis, up)
+    right_low = lax.ppermute(block[:half], axis, down)
+    far = [lax.ppermute(left_low, axis, up), lax.ppermute(right_high, axis, down)]
+    return [block, [left_low, left_high], far, [right_low, right_high]]
+
+
+def block_product(row_block, col_block):
+    if not isinstance(row_block, list):
+        row_block = [row_block[: row_block.shape[0] // 2], row_block[row_block.shape[0] // 2 :]]
+    if not isinstance(col_block, list):
+        col_block = [col_block[: col_block.shape[0] // 2], col_block[col_block.shape[0] // 2 :]]
+    return contract(row_block[0], col_block[0]) + contract(row_block[1], col_block[1])
 
 
 def two_bit_xor(a, b):
@@ -186,7 +189,9 @@
     )
     rows = square_gather(snapshots, "c")
     cols = ring_gather(panel, "r")
-    partial_value = contract(rows, cols)
+    partial_value = jnp.concatenate(
+        [jnp.concatenate([block_product(a, b) for b in cols], 1) for a in rows], 0
+    )
     placed = scatter_to_owners(partial_value, side, tiles)
     total_nodes = node_rows * tiles
     return placed / math.sqrt(total_nodes)

time: 219 us -> 221 us (level)
  waiting for transfers between devices: 140 us -> 90.8 us
  starting transfers between devices: 20.5 us -> 43 us
  matrix products: 6.31 us -> 25.6 us
  Pallas kernels: 44.3 us -> 53.7 us
    ppermute x8 -> x12, waiting for transfers between devices: 138 us -> 86.1 us  [the longest x1 25.7 us: square_gather(): z_low = lax.ppermute(block[:half], axis, to_z)]
    ppermute x8 -> x12, starting transfers between devices: 16.6 us -> 38.2 us  [the longest x2 19 us: square_gather(): corner = [lax.ppermute(x_low, axis, to_z), lax.ppermute(z_high, axis, to_x)]]
    dot_general x1 -> x32, matrix products: 6.31 us -> 25.6 us  [contract(): lax.dot_general(left, right, (((0,), (0,)), ((), ())), precision=lax.Prec...]
    pallas_call x1, Pallas kernels: 44.3 us -> 53.7 us  [scatter_to_owners(): pl.pallas_call(functools.partial(owners_kernel, side, tiles), out_shape=j...]
    ppermute x2, waiting for transfers between devices: 1.67 us -> 4.72 us  [passed_along(): lax.ppermute(value, axis, [(source, source + steps) for source in range(f...]
  transfers between devices with their start and end apart: 10 -> 14, of which waited for: 7 -> 8; matrix products, arithmetic and copies ran while one was open for 1% -> 12% of each run, Pallas kernels for 0% -> 0%
where the time goes in v7:
time: 221 us
  waiting for transfers between devices  90.8 us (41%)
  Pallas kernels  53.7 us (24%)
  starting transfers between devices  43 us (19%)
  matrix products  25.6 us (12%)
  other arithmetic  5.33 us (2%)
    pallas_call x1, Pallas kernels, scatter_to_owners(): pl.pallas_call(functools.partial(owners_kernel, side, tiles), out_shape=j...  53.7 us
    ppermute x1, waiting for transfers between devices, square_gather(): z_low = lax.ppermute(block[:half], axis, to_z)  25.7 us
    dot_general x32, matrix products, contract(): lax.dot_general(left, right, (((0,), (0,)), ((), ())), precision=lax.Prec...  25.6 us
    ppermute x2, waiting for transfers between devices, square_gather(): corner = [lax.ppermute(x_low, axis, to_z), lax.ppermute(z_high, axis, to_x)]  22.2 us
    ppermute x2, starting transfers between devices, square_gather(): corner = [lax.ppermute(x_low, axis, to_z), lax.ppermute(z_high, axis, to_x)]  19 us
    ppermute x1, waiting for transfers between devices, ring_gather(): lax.ppermute(left_low, axis, up)  15.2 us
    ppermute x1, waiting for transfers between devices, ring_gather(): left_low = lax.ppermute(block[:half], axis, up)  11.9 us
    ppermute x1, waiting for transfers between devices, square_gather(): x_low = lax.ppermute(block[:half], axis, to_x)  10 us
  transfers between devices with their start and end apart: 14, of which 8 were waited for; matrix products, arithmetic and copies ran while one was open for 12% of the time, Pallas kernels for 0%

profile of v7, /device:TPU:31, one launch (start us, length us, event | category | flops | bytes accessed | tf_op | source)
XLA Modules:
  0.0 220.5 jit_solution(5348171122055906826)
XLA Ops:
  0.0 1.6 fusion.30
  1.6 1.2 collective-permute-start.9
  2.8 1.6 collective-permute-start.11
  4.5 1.8 collective-permute-start.8
  6.3 3.5 %collective-permute-start = (f32[512,128]{1,0:T(8,128)S(1)}, f32[512,128]{1,0:T(8,128)S(1)}, u32[]{:S(2)}, u32[]{:S(2)}) collective-permute-start(f32[512,128]{1,0:T(8,128)S(1)} %slice.68), channel_id=1, source_target_pairs={{1,0},{2,1},{3,2},{4,3},{5,4},{6,5},{7,6},{8,7},{9,8},{10,9},{11,1... | collective-permute-start | bytes 786440 | tf_op jit(solution)/shard_map/ppermute | solution.py:16
  10.0 1.0 collective-permute-done
  11.8 1.3 add_multiply_fusion.2
  13.1 1.3 collective-permute-start.1
  15.0 3.7 %collective-permute-done.1 = f32[512,128]{1,0:T(8,128)S(1)} collective-permute-done((f32[512,128]{1,0:T(8,128)S(1)}, f32[512,128]{1,0:T(8,128)S(1)}, u32[]{:S(2)}, u32[]{:S(2)}) %collective-permute-start.1) | collective-permute-done | bytes 262176 | tf_op jit(solution)/shard_map/ppermute | solution.py:16
  18.8 3.0 %collective-permute-start.3 = (f32[1536,128]{1,0:T(8,128)S(1)}, f32[1536,128]{1,0:T(8,128)S(1)}, u32[]{:S(2)}, u32[]{:S(2)}) collective-permute-start(f32[1536,128]{1,0:T(8,128)S(1)} %bitcast.99), channel_id=1, source_target_pairs={{0,64},{64,128},{128,192},{192,0},{1,65},{65,129},{129,193},{193,1... | collective-permute-start | bytes 2359304 | tf_op jit(solution)/shard_map/ppermute | solution.py:79
  22.6 0.8 fusion.16
  23.5 4.2 %collective-permute-start.5 = (f32[1536,128]{1,0:T(8,128)S(1)}, f32[1536,128]{1,0:T(8,128)S(1)}, u32[]{:S(2)}, u32[]{:S(2)}) collective-permute-start(f32[1536,128]{1,0:T(8,128)S(1)} %bitcast.101), channel_id=1, source_target_pairs={{0,192},{64,0},{128,64},{192,128},{1,193},{65,1},{129,65},{193,129... | collective-permute-start | bytes 2359304 | tf_op jit(solution)/shard_map/ppermute | solution.py:78
  27.6 0.8 fusion.31
  28.4 10.0 %collective-permute-done.8 = f32[1536,128]{1,0:T(8,128)S(1)} collective-permute-done((f32[1536,128]{1,0:T(8,128)S(1)}, f32[1536,128]{1,0:T(8,128)S(1)}, u32[]{:S(2)}, u32[]{:S(2)}) %collective-permute-start.8) | collective-permute-done | bytes 786464 | tf_op jit(solution)/shard_map/ppermute | solution.py:65
  38.5 3.0 %collective-permute-start.2 = (f32[1536,128]{1,0:T(8,128)S(1)}, f32[1536,128]{1,0:T(8,128)S(1)}, u32[]{:S(2)}, u32[]{:S(2)}) collective-permute-start(f32[1536,128]{1,0:T(8,128)S(1)} %bitcast.106), channel_id=1, source_target_pairs={{0,64},{64,128},{128,192},{192,0},{1,65},{65,129},{129,193},{193,1... | collective-permute-start | bytes 2359304 | tf_op jit(solution)/shard_map/ppermute | solution.py:77
  42.3 3.1 %collective-permute-start.7 = (f32[1536,128]{1,0:T(8,128)S(1)}, f32[1536,128]{1,0:T(8,128)S(1)}, u32[]{:S(2)}, u32[]{:S(2)}) collective-permute-start(f32[1536,128]{1,0:T(8,128)S(1)} %bitcast.108), channel_id=1, source_target_pairs={{0,192},{64,0},{128,64},{192,128},{1,193},{65,1},{129,65},{193,129... | collective-permute-start | bytes 2359304 | tf_op jit(solution)/shard_map/ppermute | solution.py:80
  45.4 0.8 fusion.35
  46.2 25.7 %collective-permute-done.10 = f32[1536,128]{1,0:T(8,128)S(1)} collective-permute-done((f32[1536,128]{1,0:T(8,128)S(1)}, f32[1536,128]{1,0:T(8,128)S(1)}, u32[]{:S(2)}, u32[]{:S(2)}) %collective-permute-start.10) | collective-permute-done | bytes 786464 | tf_op jit(solution)/shard_map/ppermute | solution.py:68
  71.8 1.8 collective-permute-start.13
  74.5 17.2 %collective-permute-start.12 = (f32[1536,128]{1,0:T(8,128)S(1)}, f32[1536,128]{1,0:T(8,128)S(1)}, u32[]{:S(2)}, u32[]{:S(2)}) collective-permute-start(f32[1536,128]{1,0:T(8,128)S(1)} %collective-permute-done.8), channel_id=1, source_target_pairs={{0,32},{16,48},{32,0},{48,16},{1,33},{17,49},{33,1},{49,17},{2,34}... | collective-permute-start | bytes 2359304 | tf_op jit(solution)/shard_map/ppermute | solution.py:69
  92.5 1.1 collective-permute-done.3
  93.6 1.2 collective-permute-start.6
  98.8 11.9 %collective-permute-done.2 = f32[1536,128]{1,0:T(8,128)S(1)} collective-permute-done((f32[1536,128]{1,0:T(8,128)S(1)}, f32[1536,128]{1,0:T(8,128)S(1)}, u32[]{:S(2)}, u32[]{:S(2)}) %collective-permute-start.2) | collective-permute-done | bytes 786464 | tf_op jit(solution)/shard_map/ppermute | solution.py:77
  113.8 0.8 fusion.7
  115.4 0.8 fusion.39
  117.0 22.2 %collective-permute-done.12 = f32[1536,128]{1,0:T(8,128)S(1)} collective-permute-done((f32[1536,128]{1,0:T(8,128)S(1)}, f32[1536,128]{1,0:T(8,128)S(1)}, u32[]{:S(2)}, u32[]{:S(2)}) %collective-permute-start.12) | collective-permute-done | bytes 786464 | tf_op jit(solution)/shard_map/ppermute | solution.py:69
  140.8 0.8 fusion.3
  144.8 1.1 fusion.41
  145.9 15.2 %collective-permute-done.4 = f32[1536,128]{1,0:T(8,128)S(1)} collective-permute-done((f32[1536,128]{1,0:T(8,128)S(1)}, f32[1536,128]{1,0:T(8,128)S(1)}, u32[]{:S(2)}, u32[]{:S(2)}) %collective-permute-start.4) | collective-permute-done | bytes 786464 | tf_op jit(solution)/shard_map/ppermute | solution.py:81
  164.2 1.1 maximum_maximum_fusion.part_ref
  165.3 53.7 %shard_map.37 = f32[128,128]{1,0:T(8,128)} custom-call(f32[512,512]{1,0:T(8,128)} %maximum_maximum_fusion.part_ref), custom_call_target="tpu_custom_call" | custom-call | tf_op jit(solution)/shard_map/pallas_call | solution.py:162
  219.0 1.5 broadcast_multiply_fusion
  (50 shorter events, 21.5 us)
Async XLA Ops:
  0.0 6.3 %copy-start = (f32[3072,128]{1,0:T(8,128)S(1)}, f32[3072,128]{1,0:T(8,128)}, u32[]{:S(2)}) copy-start(f32[3072,128]{1,0:T(8,128)} %param.3) | copy-start | bytes 4718596
  0.0 9.9 %copy-start.1 = (s32[6,512]{1,0:T(8,128)S(1)}, s32[6,512]{1,0:T(8,128)}, u32[]{:S(2)}) copy-start(s32[6,512]{1,0:T(8,128)} %param.4) | copy-start | bytes 36868
  0.0 9.9 %copy-start.2 = (f32[8]{0:T(128)S(1)}, f32[8]{0:T(128)}, u32[]{:S(2)}) copy-start(f32[8]{0:T(128)} %param.5) | copy-start | bytes 100
  1.6 21.9 %collective-permute-start.9 = (f32[1536,128]{1,0:T(8,128)S(1)}, f32[1536,128]{1,0:T(8,128)S(1)}, u32[]{:S(2)}, u32[]{:S(2)}) collective-permute-start(f32[1536,128]{1,0:T(8,128)S(1)} %get-tuple-element.11), channel_id=1, source_target_pairs={{0,16},{16,0},{32,48},{48,32},{1,17},{17,1},{33,49},{49,33},{2,18}... | collective-permute-start | bytes 2359304 | tf_op jit(solution)/shard_map/ppermute | solution.py:67
  2.8 39.4 %collective-permute-start.11 = (f32[1536,128]{1,0:T(8,128)S(1)}, f32[1536,128]{1,0:T(8,128)S(1)}, u32[]{:S(2)}, u32[]{:S(2)}) collective-permute-start(f32[1536,128]{1,0:T(8,128)S(1)} %get-tuple-element.11), channel_id=1, source_target_pairs={{0,32},{16,48},{32,0},{48,16},{1,33},{17,49},{33,1},{49,17},{2,34}... | collective-permute-start | bytes 2359304 | tf_op jit(solution)/shard_map/ppermute | solution.py:66
  4.5 34.0 %collective-permute-start.8 = (f32[1536,128]{1,0:T(8,128)S(1)}, f32[1536,128]{1,0:T(8,128)S(1)}, u32[]{:S(2)}, u32[]{:S(2)}) collective-permute-start(f32[1536,128]{1,0:T(8,128)S(1)} %get-tuple-element.10), channel_id=1, source_target_pairs={{0,16},{16,0},{32,48},{48,32},{1,17},{17,1},{33,49},{49,33},{2,18}... | collective-permute-start | bytes 2359304 | tf_op jit(solution)/shard_map/ppermute | solution.py:65
  6.3 65.5 %collective-permute-start.10 = (f32[1536,128]{1,0:T(8,128)S(1)}, f32[1536,128]{1,0:T(8,128)S(1)}, u32[]{:S(2)}, u32[]{:S(2)}) collective-permute-start(f32[1536,128]{1,0:T(8,128)S(1)} %get-tuple-element.10), channel_id=1, source_target_pairs={{0,32},{16,48},{32,0},{48,16},{1,33},{17,49},{33,1},{49,17},{2,34}... | collective-permute-start | bytes 2359304 | tf_op jit(solution)/shard_map/ppermute | solution.py:68
  6.3 4.7 %collective-permute-start = (f32[512,128]{1,0:T(8,128)S(1)}, f32[512,128]{1,0:T(8,128)S(1)}, u32[]{:S(2)}, u32[]{:S(2)}) collective-permute-start(f32[512,128]{1,0:T(8,128)S(1)} %slice.68), channel_id=1, source_target_pairs={{1,0},{2,1},{3,2},{4,3},{5,4},{6,5},{7,6},{8,7},{9,8},{10,9},{11,1... | collective-permute-start | bytes 786440 | tf_op jit(solution)/shard_map/ppermute | solution.py:16
  13.1 5.7 %collective-permute-start.1 = (f32[512,128]{1,0:T(8,128)S(1)}, f32[512,128]{1,0:T(8,128)S(1)}, u32[]{:S(2)}, u32[]{:S(2)}) collective-permute-start(f32[512,128]{1,0:T(8,128)S(1)} %add_bitcast_fusion), channel_id=1, source_target_pairs={{0,1},{1,2},{2,3},{3,4},{4,5},{5,6},{6,7},{7,8},{8,9},{9,10},{10,1... | collective-permute-start | bytes 786440 | tf_op jit(solution)/shard_map/ppermute | solution.py:16
  18.8 74.9 %collective-permute-start.3 = (f32[1536,128]{1,0:T(8,128)S(1)}, f32[1536,128]{1,0:T(8,128)S(1)}, u32[]{:S(2)}, u32[]{:S(2)}) collective-permute-start(f32[1536,128]{1,0:T(8,128)S(1)} %bitcast.99), channel_id=1, source_target_pairs={{0,64},{64,128},{128,192},{192,0},{1,65},{65,129},{129,193},{193,1... | collective-permute-start | bytes 2359304 | tf_op jit(solution)/shard_map/ppermute | solution.py:79
  23.5 51.0 %collective-permute-start.5 = (f32[1536,128]{1,0:T(8,128)S(1)}, f32[1536,128]{1,0:T(8,128)S(1)}, u32[]{:S(2)}, u32[]{:S(2)}) collective-permute-start(f32[1536,128]{1,0:T(8,128)S(1)} %bitcast.101), channel_id=1, source_target_pairs={{0,192},{64,0},{128,64},{192,128},{1,193},{65,1},{129,65},{193,129... | collective-permute-start | bytes 2359304 | tf_op jit(solution)/shard_map/ppermute | solution.py:78
  38.5 72.2 %collective-permute-start.2 = (f32[1536,128]{1,0:T(8,128)S(1)}, f32[1536,128]{1,0:T(8,128)S(1)}, u32[]{:S(2)}, u32[]{:S(2)}) collective-permute-start(f32[1536,128]{1,0:T(8,128)S(1)} %bitcast.106), channel_id=1, source_target_pairs={{0,64},{64,128},{128,192},{192,0},{1,65},{65,129},{129,193},{193,1... | collective-permute-start | bytes 2359304 | tf_op jit(solution)/shard_map/ppermute | solution.py:77
  42.3 70.0 %collective-permute-start.7 = (f32[1536,128]{1,0:T(8,128)S(1)}, f32[1536,128]{1,0:T(8,128)S(1)}, u32[]{:S(2)}, u32[]{:S(2)}) collective-permute-start(f32[1536,128]{1,0:T(8,128)S(1)} %bitcast.108), channel_id=1, source_target_pairs={{0,192},{64,0},{128,64},{192,128},{1,193},{65,1},{129,65},{193,129... | collective-permute-start | bytes 2359304 | tf_op jit(solution)/shard_map/ppermute | solution.py:80
  71.8 43.6 %collective-permute-start.13 = (f32[1536,128]{1,0:T(8,128)S(1)}, f32[1536,128]{1,0:T(8,128)S(1)}, u32[]{:S(2)}, u32[]{:S(2)}) collective-permute-start(f32[1536,128]{1,0:T(8,128)S(1)} %collective-permute-done.11), channel_id=1, source_target_pairs={{0,16},{16,0},{32,48},{48,32},{1,17},{17,1},{33,49},{49,33},{2,18}... | collective-permute-start | bytes 2359304 | tf_op jit(solution)/shard_map/ppermute | solution.py:69
  74.5 64.8 %collective-permute-start.12 = (f32[1536,128]{1,0:T(8,128)S(1)}, f32[1536,128]{1,0:T(8,128)S(1)}, u32[]{:S(2)}, u32[]{:S(2)}) collective-permute-start(f32[1536,128]{1,0:T(8,128)S(1)} %collective-permute-done.8), channel_id=1, source_target_pairs={{0,32},{16,48},{32,0},{48,16},{1,33},{17,49},{33,1},{49,17},{2,34}... | collective-permute-start | bytes 2359304 | tf_op jit(solution)/shard_map/ppermute | solution.py:69
  93.6 48.8 %collective-permute-start.6 = (f32[1536,128]{1,0:T(8,128)S(1)}, f32[1536,128]{1,0:T(8,128)S(1)}, u32[]{:S(2)}, u32[]{:S(2)}) collective-permute-start(f32[1536,128]{1,0:T(8,128)S(1)} %collective-permute-done.5), channel_id=1, source_target_pairs={{0,192},{64,0},{128,64},{192,128},{1,193},{65,1},{129,65},{193,129... | collective-permute-start | bytes 2359304 | tf_op jit(solution)/shard_map/ppermute | solution.py:81
  110.6 50.4 %collective-permute-start.4 = (f32[1536,128]{1,0:T(8,128)S(1)}, f32[1536,128]{1,0:T(8,128)S(1)}, u32[]{:S(2)}, u32[]{:S(2)}) collective-permute-start(f32[1536,128]{1,0:T(8,128)S(1)} %collective-permute-done.2), channel_id=1, source_target_pairs={{0,64},{64,128},{128,192},{192,0},{1,65},{65,129},{129,193},{193,1... | collective-permute-start | bytes 2359304 | tf_op jit(solution)/shard_map/ppermute | solution.py:81

commit v8 on v7

--- a/solution.py
+++ b/solution.py
@@ -187,8 +187,8 @@
     panel = jnp.concatenate([inner[:1] + carried[None], inner[1:]], 0).reshape(
         node_rows, group_cols
     )
-    rows = square_gather(snapshots, "c")
-    cols = ring_gather(panel, "r")
+    rows = square_gather(panel, "c")
+    cols = ring_gather(snapshots, "r")
     partial_value = jnp.concatenate(
         [jnp.concatenate([block_product(a, b) for b in cols], 1) for a in rows], 0
     )

time: 221 us -> 204 us (0.923)
  starting transfers between devices: 43 us -> 63.5 us
  waiting for transfers between devices: 90.8 us -> 70.8 us
  Pallas kernels: 53.7 us -> 36.2 us
    ppermute x1, waiting for transfers between devices: 0.01 us -> 27.8 us  [square_gather(): z_high = lax.ppermute(block[half:], axis, to_z)]
    ppermute x1, starting transfers between devices: 1.64 us -> 28.5 us  [square_gather(): z_high = lax.ppermute(block[half:], axis, to_z)]
    ppermute x2, starting transfers between devices: 19 us -> 1.44 us  [square_gather(): corner = [lax.ppermute(x_low, axis, to_z), lax.ppermute(z_high, axis, to_x)]]
    pallas_call x1, Pallas kernels: 53.7 us -> 36.2 us  [scatter_to_owners(): pl.pallas_call(functools.partial(owners_kernel, side, tiles), out_shape=j...]
    ppermute x1, waiting for transfers between devices: 25.7 us -> 10.6 us  [square_gather(): z_low = lax.ppermute(block[:half], axis, to_z)]
    ppermute x1, starting transfers between devices: 0.01 us -> 14 us  [square_gather(): z_low = lax.ppermute(block[:half], axis, to_z)]
    ppermute x2, waiting for transfers between devices: 22.2 us -> 10.1 us  [square_gather(): corner = [lax.ppermute(x_low, axis, to_z), lax.ppermute(z_high, axis, to_x)]]
    ppermute x1, waiting for transfers between devices: 11.9 us -> 0.01 us  [ring_gather(): left_low = lax.ppermute(block[:half], axis, up)]
  transfers between devices with their start and end apart: 14 -> 14, of which waited for: 8 -> 7; matrix products, arithmetic and copies ran while one was open for 12% -> 13% of each run, Pallas kernels for 0% -> 0%
where the time goes in v8:
time: 204 us
  waiting for transfers between devices  70.8 us (35%)
  starting transfers between devices  63.5 us (31%)
  Pallas kernels  36.2 us (18%)
  matrix products  25.8 us (13%)
  other arithmetic  5.33 us (3%)
    pallas_call x1, Pallas kernels, scatter_to_owners(): pl.pallas_call(functools.partial(owners_kernel, side, tiles), out_shape=j...  36.2 us
    ppermute x1, starting transfers between devices, square_gather(): z_high = lax.ppermute(block[half:], axis, to_z)  28.5 us
    ppermute x1, waiting for transfers between devices, square_gather(): z_high = lax.ppermute(block[half:], axis, to_z)  27.8 us
    dot_general x32, matrix products, contract(): lax.dot_general(left, right, (((0,), (0,)), ((), ())), precision=lax.Prec...  25.8 us
    ppermute x1, starting transfers between devices, square_gather(): z_low = lax.ppermute(block[:half], axis, to_z)  14 us
    ppermute x1, waiting for transfers between devices, ring_gather(): lax.ppermute(left_low, axis, up)  13 us
    ppermute x1, waiting for transfers between devices, square_gather(): z_low = lax.ppermute(block[:half], axis, to_z)  10.6 us
    ppermute x2, waiting for transfers between devices, square_gather(): corner = [lax.ppermute(x_low, axis, to_z), lax.ppermute(z_high, axis, to_x)]  10.1 us
  transfers between devices with their start and end apart: 14, of which 7 were waited for; matrix products, arithmetic and copies ran while one was open for 13% of the time, Pallas kernels for 0%

profile of v8, /device:TPU:31, one launch (start us, length us, event | category | flops | bytes accessed | tf_op | source)
XLA Modules:
  0.0 203.6 jit_solution(2138485027638384135)
XLA Ops:
  0.0 1.6 fusion.14
  1.6 3.1 %collective-permute-start.3 = (f32[1536,128]{1,0:T(8,128)S(1)}, f32[1536,128]{1,0:T(8,128)S(1)}, u32[]{:S(2)}, u32[]{:S(2)}) collective-permute-start(f32[1536,128]{1,0:T(8,128)S(1)} %get-tuple-element.11), channel_id=1, source_target_pairs={{0,64},{64,128},{128,192},{192,0},{1,65},{65,129},{129,193},{193,1... | collective-permute-start | bytes 2359304 | tf_op jit(solution)/shard_map/ppermute | solution.py:79
  4.7 3.1 %collective-permute-start.5 = (f32[1536,128]{1,0:T(8,128)S(1)}, f32[1536,128]{1,0:T(8,128)S(1)}, u32[]{:S(2)}, u32[]{:S(2)}) collective-permute-start(f32[1536,128]{1,0:T(8,128)S(1)} %get-tuple-element.11), channel_id=1, source_target_pairs={{0,192},{64,0},{128,64},{192,128},{1,193},{65,1},{129,65},{193,129... | collective-permute-start | bytes 2359304 | tf_op jit(solution)/shard_map/ppermute | solution.py:78
  7.8 1.1 collective-permute-start.2
  8.9 2.5 %collective-permute-start.7 = (f32[1536,128]{1,0:T(8,128)S(1)}, f32[1536,128]{1,0:T(8,128)S(1)}, u32[]{:S(2)}, u32[]{:S(2)}) collective-permute-start(f32[1536,128]{1,0:T(8,128)S(1)} %get-tuple-element.10), channel_id=1, source_target_pairs={{0,192},{64,0},{128,64},{192,128},{1,193},{65,1},{129,65},{193,129... | collective-permute-start | bytes 2359304 | tf_op jit(solution)/shard_map/ppermute | solution.py:80
  11.4 3.4 %collective-permute-start = (f32[512,128]{1,0:T(8,128)S(1)}, f32[512,128]{1,0:T(8,128)S(1)}, u32[]{:S(2)}, u32[]{:S(2)}) collective-permute-start(f32[512,128]{1,0:T(8,128)S(1)} %slice.68), channel_id=1, source_target_pairs={{1,0},{2,1},{3,2},{4,3},{5,4},{6,5},{7,6},{8,7},{9,8},{10,9},{11,1... | collective-permute-start | bytes 786440 | tf_op jit(solution)/shard_map/ppermute | solution.py:16
  15.0 1.0 collective-permute-done
  16.7 1.3 add_multiply_fusion.2
  18.0 1.3 collective-permute-start.1
  20.0 3.7 %collective-permute-done.1 = f32[512,128]{1,0:T(8,128)S(1)} collective-permute-done((f32[512,128]{1,0:T(8,128)S(1)}, f32[512,128]{1,0:T(8,128)S(1)}, u32[]{:S(2)}, u32[]{:S(2)}) %collective-permute-start.1) | collective-permute-done | bytes 262176 | tf_op jit(solution)/shard_map/ppermute | solution.py:16
  23.7 1.1 collective-permute-start.9
  25.7 0.8 convolution_add_fusion.15
  26.6 4.7 %collective-permute-done.3 = f32[1536,128]{1,0:T(8,128)S(1)} collective-permute-done((f32[1536,128]{1,0:T(8,128)S(1)}, f32[1536,128]{1,0:T(8,128)S(1)}, u32[]{:S(2)}, u32[]{:S(2)}) %collective-permute-start.3) | collective-permute-done | bytes 786464 | tf_op jit(solution)/shard_map/ppermute | solution.py:79
  31.2 28.5 %collective-permute-start.11 = (f32[1536,128]{1,0:T(8,128)S(1)}, f32[1536,128]{1,0:T(8,128)S(1)}, u32[]{:S(2)}, u32[]{:S(2)}) collective-permute-start(f32[1536,128]{1,0:T(8,128)S(1)} %bitcast.69), channel_id=1, source_target_pairs={{0,32},{16,48},{32,0},{48,16},{1,33},{17,49},{33,1},{49,17},{2,34}... | collective-permute-start | bytes 2359304 | tf_op jit(solution)/shard_map/ppermute | solution.py:66
  59.7 0.8 fusion.15
  60.6 1.2 collective-permute-start.8
  61.8 0.8 fusion.17
  62.6 14.0 %collective-permute-start.10 = (f32[1536,128]{1,0:T(8,128)S(1)}, f32[1536,128]{1,0:T(8,128)S(1)}, u32[]{:S(2)}, u32[]{:S(2)}) collective-permute-start(f32[1536,128]{1,0:T(8,128)S(1)} %bitcast.75), channel_id=1, source_target_pairs={{0,32},{16,48},{32,0},{48,16},{1,33},{17,49},{33,1},{49,17},{2,34}... | collective-permute-start | bytes 2359304 | tf_op jit(solution)/shard_map/ppermute | solution.py:68
  77.4 2.3 %collective-permute-start.6 = (f32[1536,128]{1,0:T(8,128)S(1)}, f32[1536,128]{1,0:T(8,128)S(1)}, u32[]{:S(2)}, u32[]{:S(2)}) collective-permute-start(f32[1536,128]{1,0:T(8,128)S(1)} %collective-permute-done.5), channel_id=1, source_target_pairs={{0,192},{64,0},{128,64},{192,128},{1,193},{65,1},{129,65},{193,129... | collective-permute-start | bytes 2359304 | tf_op jit(solution)/shard_map/ppermute | solution.py:81
  83.4 27.8 %collective-permute-done.11 = f32[1536,128]{1,0:T(8,128)S(1)} collective-permute-done((f32[1536,128]{1,0:T(8,128)S(1)}, f32[1536,128]{1,0:T(8,128)S(1)}, u32[]{:S(2)}, u32[]{:S(2)}) %collective-permute-start.11) | collective-permute-done | bytes 786464 | tf_op jit(solution)/shard_map/ppermute | solution.py:66
  111.1 1.1 collective-permute-start.13
  115.0 0.8 convolution_add_fusion.11
  115.8 0.8 convolution_add_fusion.10
  117.4 10.6 %collective-permute-done.10 = f32[1536,128]{1,0:T(8,128)S(1)} collective-permute-done((f32[1536,128]{1,0:T(8,128)S(1)}, f32[1536,128]{1,0:T(8,128)S(1)}, u32[]{:S(2)}, u32[]{:S(2)}) %collective-permute-start.10) | collective-permute-done | bytes 786464 | tf_op jit(solution)/shard_map/ppermute | solution.py:68
  128.8 0.8 convolution_add_fusion.6
  130.4 0.8 fusion.16
  132.0 13.0 %collective-permute-done.4 = f32[1536,128]{1,0:T(8,128)S(1)} collective-permute-done((f32[1536,128]{1,0:T(8,128)S(1)}, f32[1536,128]{1,0:T(8,128)S(1)}, u32[]{:S(2)}, u32[]{:S(2)}) %collective-permute-start.4) | collective-permute-done | bytes 786464 | tf_op jit(solution)/shard_map/ppermute | solution.py:81
  150.6 1.0 fusion.26
  151.6 10.1 %collective-permute-done.12 = f32[1536,128]{1,0:T(8,128)S(1)} collective-permute-done((f32[1536,128]{1,0:T(8,128)S(1)}, f32[1536,128]{1,0:T(8,128)S(1)}, u32[]{:S(2)}, u32[]{:S(2)}) %collective-permute-start.12) | collective-permute-done | bytes 786464 | tf_op jit(solution)/shard_map/ppermute | solution.py:69
  164.9 1.1 maximum_maximum_fusion.part_ref
  165.9 36.2 %shard_map.37 = f32[128,128]{1,0:T(8,128)} custom-call(f32[512,512]{1,0:T(8,128)} %maximum_maximum_fusion.part_ref), custom_call_target="tpu_custom_call" | custom-call | tf_op jit(solution)/shard_map/pallas_call | solution.py:162
  202.2 1.5 broadcast_multiply_fusion
  (50 shorter events, 21.5 us)
Async XLA Ops:
  0.0 11.4 %copy-start = (f32[3072,128]{1,0:T(8,128)S(1)}, f32[3072,128]{1,0:T(8,128)}, u32[]{:S(2)}) copy-start(f32[3072,128]{1,0:T(8,128)} %param.3) | copy-start | bytes 4718596
  0.0 14.8 %copy-start.1 = (s32[6,512]{1,0:T(8,128)S(1)}, s32[6,512]{1,0:T(8,128)}, u32[]{:S(2)}) copy-start(s32[6,512]{1,0:T(8,128)} %param.4) | copy-start | bytes 36868
  0.0 14.8 %copy-start.2 = (f32[8]{0:T(128)S(1)}, f32[8]{0:T(128)}, u32[]{:S(2)}) copy-start(f32[8]{0:T(128)} %param.5) | copy-start | bytes 100
  1.6 29.6 %collective-permute-start.3 = (f32[1536,128]{1,0:T(8,128)S(1)}, f32[1536,128]{1,0:T(8,128)S(1)}, u32[]{:S(2)}, u32[]{:S(2)}) collective-permute-start(f32[1536,128]{1,0:T(8,128)S(1)} %get-tuple-element.11), channel_id=1, source_target_pairs={{0,64},{64,128},{128,192},{192,0},{1,65},{65,129},{129,193},{193,1... | collective-permute-start | bytes 2359304 | tf_op jit(solution)/shard_map/ppermute | solution.py:79
  4.7 55.9 %collective-permute-start.5 = (f32[1536,128]{1,0:T(8,128)S(1)}, f32[1536,128]{1,0:T(8,128)S(1)}, u32[]{:S(2)}, u32[]{:S(2)}) collective-permute-start(f32[1536,128]{1,0:T(8,128)S(1)} %get-tuple-element.11), channel_id=1, source_target_pairs={{0,192},{64,0},{128,64},{192,128},{1,193},{65,1},{129,65},{193,129... | collective-permute-start | bytes 2359304 | tf_op jit(solution)/shard_map/ppermute | solution.py:78
  7.8 54.8 %collective-permute-start.2 = (f32[1536,128]{1,0:T(8,128)S(1)}, f32[1536,128]{1,0:T(8,128)S(1)}, u32[]{:S(2)}, u32[]{:S(2)}) collective-permute-start(f32[1536,128]{1,0:T(8,128)S(1)} %get-tuple-element.10), channel_id=1, source_target_pairs={{0,64},{64,128},{128,192},{192,0},{1,65},{65,129},{129,193},{193,1... | collective-permute-start | bytes 2359304 | tf_op jit(solution)/shard_map/ppermute | solution.py:77
  8.9 68.5 %collective-permute-start.7 = (f32[1536,128]{1,0:T(8,128)S(1)}, f32[1536,128]{1,0:T(8,128)S(1)}, u32[]{:S(2)}, u32[]{:S(2)}) collective-permute-start(f32[1536,128]{1,0:T(8,128)S(1)} %get-tuple-element.10), channel_id=1, source_target_pairs={{0,192},{64,0},{128,64},{192,128},{1,193},{65,1},{129,65},{193,129... | collective-permute-start | bytes 2359304 | tf_op jit(solution)/shard_map/ppermute | solution.py:80
  11.4 4.6 %collective-permute-start = (f32[512,128]{1,0:T(8,128)S(1)}, f32[512,128]{1,0:T(8,128)S(1)}, u32[]{:S(2)}, u32[]{:S(2)}) collective-permute-start(f32[512,128]{1,0:T(8,128)S(1)} %slice.68), channel_id=1, source_target_pairs={{1,0},{2,1},{3,2},{4,3},{5,4},{6,5},{7,6},{8,7},{9,8},{10,9},{11,1... | collective-permute-start | bytes 786440 | tf_op jit(solution)/shard_map/ppermute | solution.py:16
  18.0 5.7 %collective-permute-start.1 = (f32[512,128]{1,0:T(8,128)S(1)}, f32[512,128]{1,0:T(8,128)S(1)}, u32[]{:S(2)}, u32[]{:S(2)}) collective-permute-start(f32[512,128]{1,0:T(8,128)S(1)} %add_bitcast_fusion), channel_id=1, source_target_pairs={{0,1},{1,2},{2,3},{3,4},{4,5},{5,6},{6,7},{7,8},{8,9},{9,10},{10,1... | collective-permute-start | bytes 786440 | tf_op jit(solution)/shard_map/ppermute | solution.py:16
  23.7 56.8 %collective-permute-start.9 = (f32[1536,128]{1,0:T(8,128)S(1)}, f32[1536,128]{1,0:T(8,128)S(1)}, u32[]{:S(2)}, u32[]{:S(2)}) collective-permute-start(f32[1536,128]{1,0:T(8,128)S(1)} %bitcast.67), channel_id=1, source_target_pairs={{0,16},{16,0},{32,48},{48,32},{1,17},{17,1},{33,49},{49,33},{2,18}... | collective-permute-start | bytes 2359304 | tf_op jit(solution)/shard_map/ppermute | solution.py:67
  31.2 79.9 %collective-permute-start.11 = (f32[1536,128]{1,0:T(8,128)S(1)}, f32[1536,128]{1,0:T(8,128)S(1)}, u32[]{:S(2)}, u32[]{:S(2)}) collective-permute-start(f32[1536,128]{1,0:T(8,128)S(1)} %bitcast.69), channel_id=1, source_target_pairs={{0,32},{16,48},{32,0},{48,16},{1,33},{17,49},{33,1},{49,17},{2,34}... | collective-permute-start | bytes 2359304 | tf_op jit(solution)/shard_map/ppermute | solution.py:66
  60.6 54.1 %collective-permute-start.8 = (f32[1536,128]{1,0:T(8,128)S(1)}, f32[1536,128]{1,0:T(8,128)S(1)}, u32[]{:S(2)}, u32[]{:S(2)}) collective-permute-start(f32[1536,128]{1,0:T(8,128)S(1)} %bitcast.74), channel_id=1, source_target_pairs={{0,16},{16,0},{32,48},{48,32},{1,17},{17,1},{33,49},{49,33},{2,18}... | collective-permute-start | bytes 2359304 | tf_op jit(solution)/shard_map/ppermute | solution.py:65
  62.6 65.4 %collective-permute-start.10 = (f32[1536,128]{1,0:T(8,128)S(1)}, f32[1536,128]{1,0:T(8,128)S(1)}, u32[]{:S(2)}, u32[]{:S(2)}) collective-permute-start(f32[1536,128]{1,0:T(8,128)S(1)} %bitcast.75), channel_id=1, source_target_pairs={{0,32},{16,48},{32,0},{48,16},{1,33},{17,49},{33,1},{49,17},{2,34}... | collective-permute-start | bytes 2359304 | tf_op jit(solution)/shard_map/ppermute | solution.py:68
  77.4 53.0 %collective-permute-start.6 = (f32[1536,128]{1,0:T(8,128)S(1)}, f32[1536,128]{1,0:T(8,128)S(1)}, u32[]{:S(2)}, u32[]{:S(2)}) collective-permute-start(f32[1536,128]{1,0:T(8,128)S(1)} %collective-permute-done.5), channel_id=1, source_target_pairs={{0,192},{64,0},{128,64},{192,128},{1,193},{65,1},{129,65},{193,129... | collective-permute-start | bytes 2359304 | tf_op jit(solution)/shard_map/ppermute | solution.py:81
  80.5 64.5 %collective-permute-start.4 = (f32[1536,128]{1,0:T(8,128)S(1)}, f32[1536,128]{1,0:T(8,128)S(1)}, u32[]{:S(2)}, u32[]{:S(2)}) collective-permute-start(f32[1536,128]{1,0:T(8,128)S(1)} %collective-permute-done.2), channel_id=1, source_target_pairs={{0,64},{64,128},{128,192},{192,0},{1,65},{65,129},{129,193},{193,1... | collective-permute-start | bytes 2359304 | tf_op jit(solution)/shard_map/ppermute | solution.py:81
  111.1 37.0 %collective-permute-start.13 = (f32[1536,128]{1,0:T(8,128)S(1)}, f32[1536,128]{1,0:T(8,128)S(1)}, u32[]{:S(2)}, u32[]{:S(2)}) collective-permute-start(f32[1536,128]{1,0:T(8,128)S(1)} %collective-permute-done.11), channel_id=1, source_target_pairs={{0,16},{16,0},{32,48},{48,32},{1,17},{17,1},{33,49},{49,33},{2,18}... | collective-permute-start | bytes 2359304 | tf_op jit(solution)/shard_map/ppermute | solution.py:69
  114.7 47.0 %collective-permute-start.12 = (f32[1536,128]{1,0:T(8,128)S(1)}, f32[1536,128]{1,0:T(8,128)S(1)}, u32[]{:S(2)}, u32[]{:S(2)}) collective-permute-start(f32[1536,128]{1,0:T(8,128)S(1)} %collective-permute-done.8), channel_id=1, source_target_pairs={{0,32},{16,48},{32,0},{48,16},{1,33},{17,49},{33,1},{49,17},{2,34}... | collective-permute-start | bytes 2359304 | tf_op jit(solution)/shard_map/ppermute | solution.py:69
